TPU v7x, 32 devices: a whole 2x2x4 slice. The times are simulated.
32 devices in a mesh: section: 4 (over x, core), dom: 8 (over z, y).
Axes of the slice: x: 2, y: 2, z: 4, core: 2. Of those that a mesh axis runs over, the one named last changes fastest.
Arguments:
- node_latents: bfloat16 [4, 8192, 512], P('section', 'dom'), may hold values from -6 to 6
- edge_latents: bfloat16 [4, 12288, 512], P('section', 'dom'), may hold values from -6 to 6
- entering_nodes: bfloat16 [8192, 512], P('dom'), may hold values from -6 to 6
- entering_edges: bfloat16 [12288, 512], P('dom'), may hold values from -6 to 6
- edge_first: bfloat16 [4, 1536, 512], P('section'), may hold values from -0.15625 to 0.15625
- edge_second: bfloat16 [4, 512, 512], P('section'), may hold values from -0.25 to 0.25
- edge_gain: float32 [4, 512], P('section'), may hold values from 0.1 to 1.9
- node_first: bfloat16 [4, 1024, 512], P('section'), may hold values from -0.1875 to 0.1875
- node_second: bfloat16 [4, 512, 512], P('section'), may hold values from -0.25 to 0.25
- node_gain: float32 [4, 512], P('section'), may hold values from 0.1 to 1.9
- pair_list: int32 [8, 12, 3], P('dom'), may hold values from 0 to 7, as said below
- send_list: int32 [8, 4], P('dom'), may hold values from 0 to 7, as said below
- senders: int32 [12288, 128], P('dom'), may hold values from 0 to 1, as said below
- receivers: int32 [12288, 128], P('dom'), may hold values from 0 to 1, as said below
Outputs:
- final_nodes: bfloat16 [4, 8192, 512], P('section', 'dom')
- final_edges: bfloat16 [4, 12288, 512], P('section', 'dom')
Inputs may be any that keep to these rules, and one draw needn't show every extreme that they name: `pair_list`: columns 0 and 2 are node block numbers below 8, column 1 a partner code 0 to 4 (0: sender block on the same partition); every partition lists each code 1 to 4 at least once and names each of its node blocks in column 0 at least once. `send_list`: node block numbers below 8. `senders`: each row has exactly one 1. `receivers`: each row has exactly one 1.
All inputs are finite; a program needn't handle non-finite values.
Results may differ from a plain program's by a relative error of at most 0.0075.
Values may be sent and summed in bfloat16 or wider, within the bound.
No kernel may reach another device: no remote copies, remote signals or barrier semaphores. Data moves between devices by JAX's collectives and lax.ppermute only.
A program may use at most 128 MiB of HBM per device.

v0:
```python
import jax
import jax.numpy as jnp
from jax import lax
from jax.experimental import pallas as pl
from jax.experimental.pallas import tpu as pltpu
from jax.sharding import PartitionSpec as P


partner_offsets = (1, -1, 2, -2)
partners = len(partner_offsets)
epsilon = 1e-05
f32 = jnp.float32
bf16 = jnp.bfloat16
VMEM = pl.BlockSpec(memory_space=pltpu.VMEM)
SMEM = pl.BlockSpec(memory_space=pltpu.SMEM)
HBM = pl.BlockSpec(memory_space=pltpu.HBM)
group = 3


def rotated(block, axis, distance):
    devices = range(lax.axis_size(axis))
    route = [((i - distance) % len(devices), i) for i in devices]
    return lax.ppermute(block, axis, route)


def layer_norm(values, gain):
    centred = values - jnp.mean(values, axis=-1, keepdims=True)
    spread = jnp.mean(centred * centred, axis=-1, keepdims=True)
    return centred * lax.rsqrt(spread + epsilon) * gain


def product(left, right):
    return jnp.dot(left, right, preferred_element_type=f32)


def shape(dims, kind):
    return jax.ShapeDtypeStruct(dims, kind)


def call(kernel, ins, outs, scratch=(), copies=0, aliases=None, flops=0, moved=0):
    specs = {"v": VMEM, "s": SMEM, "h": HBM}
    scratch = list(scratch)
    if copies:
        scratch.append(pltpu.SemaphoreType.DMA((copies,)))
    step = pl.pallas_call(
        kernel,
        out_shape=tuple(out for _, out in outs),
        in_specs=[specs[place] for place, _ in ins],
        out_specs=tuple(specs[place] for place, _ in outs),
        scratch_shapes=scratch,
        input_output_aliases=aliases or {},
        compiler_params=pltpu.CompilerParams(vmem_limit_bytes=24 << 20),
        cost_estimate=pl.CostEstimate(flops=flops, bytes_accessed=moved, transcendentals=0),
    )
    values = [
            pltpu.with_memory_space_constraint(value, pltpu.HBM) if place == "h" else value
            for place, value in ins
    ]
    return step(*values)


def started(pairs, sems, first=0):
    copies = [
        pltpu.make_async_copy(source, target, sems.at[first + i])
        for i, (source, target) in enumerate(pairs)
    ]
    for copy in copies:
        copy.start()
    return copies


def finish(copies):
    for copy in copies:
        copy.wait()


def aligned(index, rows):
    return pl.ds(pl.multiple_of(index * rows, rows), rows)


def span(index, rows):
    return pl.ds(index * rows, rows)


def plan_kernel(sends_far, pairs_far, nodes, plan, front, back, *rest):
    outs, (near, sends, pairs, sems) = rest[:partners], rest[partners:]
    rows = outs[0].shape[0]
    blocks = nodes.shape[0] // rows
    number = pairs.shape[2]
    copies = started([(sends_far, sends), (nodes, near), (pairs_far, pairs)], sems)
    copies[0].wait()
    chosen = [sends[0, i] for i in range(partners)]
    used = []
    for block in range(blocks):
        hit = chosen[0] == block
        for index in chosen[1:]:
            hit = hit | (index == block)
        used.append(hit.astype(jnp.int32))
    ahead = jnp.int32(0)
    behind = sum(used)
    for block in range(blocks):
        place = jnp.where(used[block] == 1, ahead, behind)
        ahead = ahead + used[block]
        behind = behind + 1 - used[block]
        plan[place] = jnp.int32(block)
        plan[blocks + block] = place
    for i in range(partners):
        plan[2 * blocks + i] = plan[blocks + chosen[i]]
    copies[2].wait()
    for k in range(number):
        code = pairs[1, 0, k]
        local = plan[blocks + pairs[2, 0, k]]
        plan[2 * blocks + partners + k] = jnp.where(code == 0, local, blocks + code - 1)
        plan[2 * blocks + partners + number + k] = plan[blocks + pairs[0, 0, k]]
    copies[1].wait()
    for index, out in zip(chosen, outs):
        out[...] = near[aligned(index, rows), :]
    for i in range(partners):
        front[span(i, rows), :] = near[aligned(plan[i], rows), :]
    for i in range(partners, blocks):
        back[span(i - partners, rows), :] = near[aligned(plan[i], rows), :]


def project(front, back, w_sent, w_received, sent, received):
    rows = front.shape[0]
    for side, nodes in ((pl.ds(0, rows), front), (pl.ds(rows, back.shape[0]), back)):
        sent[side, :] = product(nodes[...], w_sent[...]).astype(bf16)
        received[side, :] = product(nodes[...], w_received[...]).astype(bf16)


def load_kernel(
    front,
    back,
    edges,
    first,
    senders,
    receivers,
    edges_one,
    edges_two,
    w_edge,
    w_sent,
    w_received,
    base_one,
    base_two,
    sent,
    received,
    ends,
    flipped,
    near_senders,
    near_receivers,
    sems,
):
    rows = senders.shape[1]
    width = front.shape[1]
    half = edges_one.shape[0]
    copies = started(
        [
            (first.at[span(1, width), :], w_sent),
            (first.at[span(2, width), :], w_received),
            (first.at[span(0, width), :], w_edge),
            (edges.at[span(0, half), :], edges_one),
            (edges.at[span(1, half), :], edges_two),
            (senders, near_senders),
            (receivers, near_receivers),
        ],
        sems,
    )
    finish(copies[:2])
    project(front, back, w_sent, w_received, sent, received)
    finish(copies[2:4])
    base_one[...] = product(edges_one[...], w_edge[...])
    copies[4].wait()
    base_two[...] = product(edges_two[...], w_edge[...])
    finish(copies[5:])
    for block in range(senders.shape[0] // rows):
        here = span(block, rows)
        for side, source in enumerate((near_senders, near_receivers)):
            part = source[here, :].astype(f32)
            ends[here, side * rows : (side + 1) * rows] = part.astype(bf16)
            flipped[span(2 * block + side, rows), :] = part.T.astype(bf16)


def project_kernel(
    front, back, edges_one, w_edge, w_sent, w_received, base_one, sent, received
):
    project(front, back, w_sent, w_received, sent, received)
    base_one[...] = product(edges_one[...], w_edge[...])


def base_kernel(edges, w_edge, base):
    base[...] = product(edges[...], w_edge[...])


def edge_kernel(plan, flag, entering, *refs):
    edge_part(plan, refs[:-1])
    new_edges = refs[partners + 11 : partners + 13]
    half = new_edges[0].shape[0]

    @pl.when(flag[0] == 1)
    def _():
        finish(
            started([(entering.at[span(i, half), :], new_edges[i]) for i in range(2)], refs[-1])
        )


def edge_last_kernel(plan, *refs):
    edge_part(plan, refs)


def edge_part(plan, refs):
    incoming, refs = refs[:partners], refs[partners:]
    base = refs[0:2]
    sent, received, ends, flipped = refs[2:6]
    edges = refs[6:8]
    w_sent, second, gain = refs[8:11]
    new_edges = refs[11:13]
    low, sums = refs[13:15]
    outs = refs[15 : 15 + partners]
    (lookup,) = refs[15 + partners :]
    rows = incoming[0].shape[0]
    blocks = sent.shape[0] // rows
    half = edges[0].shape[0]
    number = 2 * half // rows
    sources = 2 * blocks + partners
    lookup[: blocks * rows, :] = sent[...]
    for i, block in enumerate(incoming):
        lookup[span(blocks + i, rows), :] = product(block[...], w_sent[...]).astype(bf16)
    sums[...] = jnp.zeros_like(sums)
    each = half // rows
    step = group if each % group == 0 else 1
    for start in range(0, number, step):
        part, begin = divmod(start, each)
        hidden = []
        for block in range(start, start + step):
            both = jnp.concatenate(
                [
                    lookup[aligned(plan[sources + block], rows), :],
                    received[aligned(plan[sources + number + block], rows), :],
                ],
                axis=0,
            )
            summed = base[part][span(block - part * each, rows), :] + product(
                ends[span(block, rows), :], both
            )
            hidden.append(jnp.maximum(summed, 0.0).astype(bf16))
        message = layer_norm(product(jnp.concatenate(hidden, axis=0), second[...]), gain[...])
        here = pl.ds(begin * rows, step * rows)
        new_edges[part][here, :] = (edges[part][here, :].astype(f32) + message).astype(bf16)
        rounded = message.astype(bf16)
        low[pl.ds(start * rows, step * rows), :] = rounded
        for i in range(step):
            block = start + i
            spread = product(
                flipped[span(2 * block, rows), :], rounded[i * rows : (i + 1) * rows, :]
            )
            sums[aligned(plan[sources + block], rows), :] += spread
    for i, out in enumerate(outs):
        out[...] = sums[span(blocks + i, rows), :].astype(bf16)


def node_update(nodes, ready, total, w_summed, second, gain):
    hidden = jnp.maximum(ready + product(total.astype(bf16), w_summed), 0.0).astype(bf16)
    update = layer_norm(product(hidden, second[...]), gain[...])
    return (nodes[...].astype(f32) + update).astype(bf16)


def settle(plan, low, flipped, sums, front, back, first, second, gain, own, ready, total):
    rows = flipped.shape[1]
    width = front.shape[1]
    blocks = (front.shape[0] + back.shape[0]) // rows
    number = low.shape[0] // rows
    targets = 2 * blocks + partners + number
    total[...] = sums[: blocks * rows, :]
    for block in range(number):
        spread = product(flipped[span(2 * block + 1, rows), :], low[span(block, rows), :])
        total[aligned(plan[targets + block], rows), :] += spread
    kept = partners * rows
    own[...] = total[:kept, :]
    ready[...] = product(front[...], first[:width, :])
    return node_update(
        back,
        product(back[...], first[:width, :]),
        total[kept:, :],
        first[width:, :],
        second,
        gain,
    )


def settle_kernel(
    plan, flag, low, flipped, sums, front, back, first, second, gain, entering, own, ready,
    new_back, total, sems,
):
    rows = flipped.shape[1]
    blocks = (front.shape[0] + back.shape[0]) // rows
    new_back[...] = settle(
        plan, low, flipped, sums, front, back, first, second, gain, own, ready, total
    )

    @pl.when(flag[0] == 1)
    def _():
        finish(
            started(
                [
                    (
                        entering.at[aligned(plan[partners + i], rows), :],
                        new_back.at[span(i, rows), :],
                    )
                    for i in range(blocks - partners)
                ],
                sems,
            )
        )


def settle_last_kernel(
    plan, low, flipped, sums, front, back, first, second, gain, edges_one, edges_two, own, ready,
    final_nodes, final_edges, total, near, sems,
):
    rows = flipped.shape[1]
    half = edges_one.shape[0]
    blocks = (front.shape[0] + back.shape[0]) // rows
    copies = started(
        [
            (edges_one, final_edges.at[span(0, half), :]),
            (edges_two, final_edges.at[span(1, half), :]),
        ],
        sems,
    )
    near[...] = settle(
        plan, low, flipped, sums, front, back, first, second, gain, own, ready, total
    )
    copies += started(
        [
            (near.at[span(i, rows), :], final_nodes.at[aligned(plan[partners + i], rows), :])
            for i in range(blocks - partners)
        ],
        sems,
        2,
    )
    finish(copies)


def node_part(plan, returned, own, ready, front, first, second, gain, total, blocks):
    rows = returned[0].shape[0]
    total[...] = own[...]
    for i, block in enumerate(returned):
        total[aligned(plan[2 * blocks + i], rows), :] += block[...].astype(f32)
    width = front.shape[1]
    return node_update(front, ready[...], total[...], first[width:, :], second, gain)


def node_kernel(plan, flag, *refs):
    returned, refs = refs[:partners], refs[partners:]
    own, ready, front, first, second, gain, entering, new_front, total, sems = refs
    rows = returned[0].shape[0]
    blocks = entering.shape[0] // rows
    new_front[...] = node_part(
        plan, returned, own, ready, front, first, second, gain, total, blocks
    )

    @pl.when(flag[0] == 1)
    def _():
        finish(
            started(
                [
                    (entering.at[aligned(plan[i], rows), :], new_front.at[span(i, rows), :])
                    for i in range(partners)
                ],
                sems,
            )
        )


def node_last_kernel(plan, *refs):
    returned, refs = refs[:partners], refs[partners:]
    own, ready, front, first, second, gain, _, final_nodes, total, near, sems = refs
    rows = returned[0].shape[0]
    blocks = final_nodes.shape[0] // rows
    near[...] = node_part(plan, returned, own, ready, front, first, second, gain, total, blocks)
    finish(
        started(
            [
                (near.at[span(i, rows), :], final_nodes.at[aligned(plan[i], rows), :])
                for i in range(partners)
            ],
            sems,
        )
    )


def ticks(
    node_latents,
    edge_latents,
    entering_nodes,
    entering_edges,
    edge_first,
    edge_second,
    edge_gain,
    node_first,
    node_second,
    node_gain,
    pair_list,
    send_list,
    senders,
    receivers,
):
    edge_second, node_first, node_second = edge_second[0], node_first[0], node_second[0]
    last = lax.axis_index("section") == lax.axis_size("section") - 1
    flag = last.astype(jnp.int32).reshape(1)
    node_rows, width = entering_nodes.shape
    edge_rows = entering_edges.shape[0]
    rows = senders.shape[1]
    blocks = node_rows // rows
    number = edge_rows // rows
    half = edge_rows // 2
    kept, rest = partners * rows, node_rows - partners * rows
    square = 2 * width * width
    block = ("v", shape((rows, width), bf16))
    front_out = ("v", shape((kept, width), bf16))
    back_out = ("v", shape((rest, width), bf16))
    half_low = ("v", shape((half, width), bf16))
    half_wide = ("v", shape((half, width), f32))
    weight = ("v", shape((width, width), bf16))
    all_low = ("v", shape((node_rows, width), bf16))
    slots = ("v", shape((node_rows + kept, width), f32))
    front_wide = ("v", shape((kept, width), f32))

    plan, front, back, *picked = call(
        plan_kernel,
        [("h", send_list), ("h", jnp.transpose(pair_list, (2, 0, 1))), ("h", node_latents[0])],
        [("s", shape((2 * blocks + partners + 2 * number,), jnp.int32)), front_out, back_out]
        + [block] * partners,
        scratch=[pltpu.VMEM((node_rows, width), bf16), pltpu.SMEM((1, partners), jnp.int32), pltpu.SMEM((3, 1, number), jnp.int32)],
        copies=3,
        moved=1 << 20,
    )

    def fetched(picked):
        return [rotated(picked[i], "dom", partner_offsets[i]) for i in range(partners)]

    def edge_stage(kernel, extra, incoming, base, sent, received, edges):
        new_one, new_two, low, sums, *partials = call(
            kernel,
            [("s", plan)]
            + extra
            + [("v", value) for value in (*incoming, *base, sent, received, ends, flipped)]
            + [("v", value) for value in (*edges, w_sent, edge_second, edge_gain)],
            [half_low, half_low, ("v", shape((edge_rows, width), bf16)), slots]
            + [block] * partners,
            scratch=[pltpu.VMEM((node_rows + kept, width), bf16)],
            copies=2 if extra else 0,
            flops=square * 2 * edge_rows,
            moved=16 << 20,
        )
        return (new_one, new_two), low, sums, partials

    def handed_back(partials):
        return [rotated(partials[i], "dom", -partner_offsets[i]) for i in range(partners)]

    incoming = fetched(picked)
    (
        edges_one,
        edges_two,
        w_edge,
        w_sent,
        w_received,
        base_one,
        base_two,
        sent,
        received,
        ends,
        flipped,
    ) = call(
        load_kernel,
        [("v", front), ("v", back)]
        + [("h", value) for value in (edge_latents[0], edge_first[0], senders, receivers)],
        [half_low, half_low, weight, weight, weight, half_wide, half_wide]
        + [all_low, all_low]
        + [("v", shape((edge_rows, 2 * rows), bf16)), ("v", shape((2 * edge_rows, rows), bf16))],
        scratch=[pltpu.VMEM((edge_rows, rows), jnp.int32)] * 2,
        copies=7,
        flops=square * (edge_rows + 2 * node_rows),
        moved=16 << 20,
    )
    edges, low, sums, partials = edge_stage(
        edge_kernel,
        [("s", flag), ("h", entering_edges)],
        incoming,
        (base_one, base_two), sent, received, (edges_one, edges_two)
    )
    edges_one = rotated(edges[0], "section", 1)
    returned = handed_back(partials)
    own, ready, new_back = call(
        settle_kernel,
        [("s", plan), ("s", flag)]
        + [
            ("v", value)
            for value in (low, flipped, sums, front, back, node_first, node_second, node_gain)
        ]
        + [("h", entering_nodes)],
        [front_wide, front_wide, back_out],
        scratch=[pltpu.VMEM((node_rows, width), f32)],
        copies=blocks - partners,
        flops=square * 2 * node_rows,
        moved=12 << 20,
    )
    back = rotated(new_back, "section", 1)
    (new_front,) = call(
        node_kernel,
        [("s", plan), ("s", flag)]
        + [
            ("v", value)
            for value in (*returned, own, ready, front, node_first, node_second, node_gain)
        ]
        + [("h", entering_nodes)],
        [front_out],
        scratch=[pltpu.VMEM((kept, width), f32)],
        copies=partners,
        flops=square * 2 * kept,
        moved=6 << 20,
    )
    front = rotated(new_front, "section", 1)
    edges_two = rotated(edges[1], "section", 1)

    picked = call(
        lambda plan, nodes, *outs: pick(plan, nodes, outs, blocks),
        [("s", plan), ("v", front)],
        [block] * partners,
        moved=1 << 20,
    )
    incoming = fetched(picked)
    base_one, sent, received = call(
        project_kernel,
        [("v", value) for value in (front, back, edges_one, w_edge, w_sent, w_received)],
        [half_wide, all_low, all_low],
        flops=square * (half + 2 * node_rows),
        moved=8 << 20,
    )
    (base_two,) = call(
        base_kernel,
        [("v", edges_two), ("v", w_edge)],
        [half_wide],
        flops=square * half,
        moved=3 << 20,
    )
    edges, low, sums, partials = edge_stage(
        edge_last_kernel,
        [],
        incoming,
        (base_one, base_two), sent, received, (edges_one, edges_two)
    )
    returned = handed_back(partials)
    own, ready, final_nodes, final_edges = call(
        settle_last_kernel,
        [("s", plan)]
        + [
            ("v", value)
            for value in (low, flipped, sums, front, back, node_first, node_second, node_gain)
        ]
        + [("v", value) for value in edges],
        [front_wide, front_wide]
        + [("h", shape((node_rows, width), bf16)), ("h", shape((edge_rows, width), bf16))],
        scratch=[pltpu.VMEM((node_rows, width), f32), pltpu.VMEM((rest, width), bf16)],
        copies=2 + blocks - partners,
        flops=square * 2 * node_rows,
        moved=12 << 20,
    )
    (final_nodes,) = call(
        node_last_kernel,
        [("s", plan)]
        + [
            ("v", value)
            for value in (*returned, own, ready, front, node_first, node_second, node_gain)
        ]
        + [("h", final_nodes)],
        [("h", shape((node_rows, width), bf16))],
        scratch=[pltpu.VMEM((kept, width), f32), pltpu.VMEM((kept, width), bf16)],
        copies=partners,
        aliases={7 + partners: 0},
        flops=square * 2 * kept,
        moved=6 << 20,
    )
    return (final_nodes[None], final_edges[None])


def pick(plan, nodes, outs, blocks):
    rows = outs[0].shape[0]
    for i, out in enumerate(outs):
        out[...] = nodes[aligned(plan[2 * blocks + i], rows), :]


def solution(mesh):
    placed = (
        P("section", "dom", None),
        P("section", "dom", None),
        P("dom", None),
        P("dom", None),
        P("section", None, None),
        P("section", None, None),
        P("section", None),
        P("section", None, None),
        P("section", None, None),
        P("section", None),
        P("dom", None, None),
        P("dom", None),
        P("dom", None),
        P("dom", None),
    )
    return jax.shard_map(
        ticks,
        mesh=mesh,
        in_specs=placed,
        out_specs=(P("section", "dom", None), P("section", "dom", None)),
        check_vma=False,
    )
```

profile of v0, /device:TPU:6, one launch (start us, length us, event | category | flops | bytes accessed | tf_op | source)
XLA Modules:
  0.0 82.1 jit_solution(8505190592949799486)
XLA Ops:
  0.6 1.9 %shard_map.149 = (s32[44]{0:T(128)S(1)}, bf16[512,512]{1,0:T(8,128)(2,1)S(1)}, bf16[512,512]{1,0:T(8,128)(2,1)S(1)}, bf16[128,512]{1,0:T(8,128)(2,1)S(1)}, bf16[...) custom-call(s32[1,4]{1,0:T(1,128)} %sends_far.1, s32[3,1,12]{2,1,0:T(1,128)} %bitcast.22, ...), custom_call_target="tpu_custom_call" | custom-call | bytes 1048576 | tf_op jit(solution)/shard_map/pallas_call | solution.py:59
  2.5 1.6 %collective-permute-start = (bf16[128,512]{1,0:T(8,128)(2,1)S(1)}, bf16[128,512]{1,0:T(8,128)(2,1)S(1)}, u32[]{:S(2)}, u32[]{:S(2)}) collective-permute-start(bf16[128,512]{1,0:T(8,128)(2,1)S(1)} %get-tuple-element.51), channel_id=1, source_target_pairs={{7,0},{0,1},{1,2},{2,3},{3,4},{4,5},{5,6},{6,7},{15,8},{8,9},{9,10... | collective-permute-start | bytes 393224 | tf_op jit(solution)/shard_map/ppermute | solution.py:23
  4.1 0.5 collective-permute-start.1
  4.6 1.6 %collective-permute-start.2 = (bf16[128,512]{1,0:T(8,128)(2,1)S(1)}, bf16[128,512]{1,0:T(8,128)(2,1)S(1)}, u32[]{:S(2)}, u32[]{:S(2)}) collective-permute-start(bf16[128,512]{1,0:T(8,128)(2,1)S(1)} %get-tuple-element.53), channel_id=1, source_target_pairs={{6,0},{7,1},{0,2},{1,3},{2,4},{3,5},{4,6},{5,7},{14,8},{15,9},{8,1... | collective-permute-start | bytes 393224 | tf_op jit(solution)/shard_map/ppermute | solution.py:23
  6.1 2.2 %collective-permute-start.3 = (bf16[128,512]{1,0:T(8,128)(2,1)S(1)}, bf16[128,512]{1,0:T(8,128)(2,1)S(1)}, u32[]{:S(2)}, u32[]{:S(2)}) collective-permute-start(bf16[128,512]{1,0:T(8,128)(2,1)S(1)} %get-tuple-element.54), channel_id=1, source_target_pairs={{2,0},{3,1},{4,2},{5,3},{6,4},{7,5},{0,6},{1,7},{10,8},{11,9},{12,... | collective-permute-start | bytes 393224 | tf_op jit(solution)/shard_map/ppermute | solution.py:23
  8.4 0.0 copy-start.2
  8.4 0.0 copy-start.4
  8.4 4.0 %shard_map.150 = (bf16[768,512]{1,0:T(8,128)(2,1)S(1)}, bf16[768,512]{1,0:T(8,128)(2,1)S(1)}, bf16[512,512]{1,0:T(8,128)(2,1)S(1)}, bf16[512,512]{1,0:T(8,128)(2...) custom-call(bf16[512,512]{1,0:T(8,128)(2,1)S(1)} %get-tuple-element., ...), custom_call_target="tpu_custom_call" | custom-call | flops 1879048192 | bytes 16777216 | tf_op jit(solution)/shard_map/pallas_call | solution.py:59
  12.4 0.0 collective-permute-done.refs_0_
  12.4 0.0 collective-permute-done.1.refs_1_
  12.4 1.1 %collective-permute-done.2.refs_2_ = bf16[128,512]{1,0:T(8,128)(2,1)S(1)} collective-permute-done((bf16[128,512]{1,0:T(8,128)(2,1)S(1)}, bf16[128,512]{1,0:T(8,128)(2,1)S(1)}, u32[]{:S(2)}, u32[]{:S(2)}) %collective-permute-start.2) | collective-permute-done | bytes 131104 | tf_op jit(solution)/shard_map/ppermute | solution.py:23
  13.5 1.8 %collective-permute-done.3.refs_3_ = bf16[128,512]{1,0:T(8,128)(2,1)S(1)} collective-permute-done((bf16[128,512]{1,0:T(8,128)(2,1)S(1)}, bf16[128,512]{1,0:T(8,128)(2,1)S(1)}, u32[]{:S(2)}, u32[]{:S(2)}) %collective-permute-start.3) | collective-permute-done | bytes 131104 | tf_op jit(solution)/shard_map/ppermute | solution.py:23
  15.3 0.0 copy-done.2
  15.3 0.0 copy-done.4
  15.3 0.0 copy-start
  15.3 0.0 copy-start.1
  15.3 0.0 copy-start.3
  15.3 4.8 %shard_map.151 = (bf16[768,512]{1,0:T(8,128)(2,1)S(1)}, bf16[768,512]{1,0:T(8,128)(2,1)S(1)}, bf16[1536,512]{1,0:T(8,128)(2,1)S(1)}, f32[1536,512]{1,0:T(8,128)S...) custom-call(s32[44]{0:T(128)S(1)} %get-tuple-element.50.plan, ...), custom_call_target="tpu_custom_call" | custom-call | flops 1610612736 | bytes 16777216 | tf_op jit(solution)/shard_map/pallas_call | solution.py:59
  20.1 1.1 %collective-permute-start.4 = (bf16[128,512]{1,0:T(8,128)(2,1)S(1)}, bf16[128,512]{1,0:T(8,128)(2,1)S(1)}, u32[]{:S(2)}, u32[]{:S(2)}) collective-permute-start(bf16[128,512]{1,0:T(8,128)(2,1)S(1)} %get-tuple-element.66), channel_id=1, source_target_pairs={{1,0},{2,1},{3,2},{4,3},{5,4},{6,5},{7,6},{0,7},{9,8},{10,9},{11,1... | collective-permute-start | bytes 393224 | tf_op jit(solution)/shard_map/ppermute | solution.py:23
  21.2 0.1 collective-permute-start.15
  21.3 0.5 collective-permute-start.14
  21.9 2.1 %collective-permute-start.5 = (bf16[128,512]{1,0:T(8,128)(2,1)S(1)}, bf16[128,512]{1,0:T(8,128)(2,1)S(1)}, u32[]{:S(2)}, u32[]{:S(2)}) collective-permute-start(bf16[128,512]{1,0:T(8,128)(2,1)S(1)} %get-tuple-element.67), channel_id=1, source_target_pairs={{7,0},{0,1},{1,2},{2,3},{3,4},{4,5},{5,6},{6,7},{15,8},{8,9},{9,10... | collective-permute-start | bytes 393224 | tf_op jit(solution)/shard_map/ppermute | solution.py:23
  23.9 3.3 %collective-permute-start.6 = (bf16[128,512]{1,0:T(8,128)(2,1)S(1)}, bf16[128,512]{1,0:T(8,128)(2,1)S(1)}, u32[]{:S(2)}, u32[]{:S(2)}) collective-permute-start(bf16[128,512]{1,0:T(8,128)(2,1)S(1)} %get-tuple-element.68), channel_id=1, source_target_pairs={{2,0},{3,1},{4,2},{5,3},{6,4},{7,5},{0,6},{1,7},{10,8},{11,9},{12,... | collective-permute-start | bytes 393224 | tf_op jit(solution)/shard_map/ppermute | solution.py:23
  27.2 0.1 collective-permute-done.4.refs_0_
  27.3 0.6 collective-permute-start.7
  27.9 0.0 copy-done
  27.9 0.0 copy-done.1
  27.9 0.0 copy-done.3
  27.9 2.7 %shard_map.152 = (f32[512,512]{1,0:T(8,128)S(1)}, f32[512,512]{1,0:T(8,128)S(1)}, bf16[512,512]{1,0:T(8,128)(2,1)S(1)}) custom-call(s32[44]{0:T(128)S(1)} %get-tuple-element.50.plan, s32[1]{0:T(128)} %bitcast.2.flag, bf16[1536,512]{1,0:T(8,128)(2,1)S(1)} %get-tuple-element.70.low, bf16[3072,128]{1,0:T(8,128)(2,1)S(1)} %get-tuple-element.62.refs_9_.flipped, ...), custom_call_target="tpu_custom_call" | custom-call | flops 1073741824 | bytes 12582912 | tf_op jit(solution)/shard_map/pallas_call | solution.py:59
  30.6 0.0 collective-permute-done.5.refs_1_
  30.6 1.2 %collective-permute-done.6.refs_2_ = bf16[128,512]{1,0:T(8,128)(2,1)S(1)} collective-permute-done((bf16[128,512]{1,0:T(8,128)(2,1)S(1)}, bf16[128,512]{1,0:T(8,128)(2,1)S(1)}, u32[]{:S(2)}, u32[]{:S(2)}) %collective-permute-start.6) | collective-permute-done | bytes 131104 | tf_op jit(solution)/shard_map/ppermute | solution.py:23
  31.9 4.4 %collective-permute-done.7.refs_3_ = bf16[128,512]{1,0:T(8,128)(2,1)S(1)} collective-permute-done((bf16[128,512]{1,0:T(8,128)(2,1)S(1)}, bf16[128,512]{1,0:T(8,128)(2,1)S(1)}, u32[]{:S(2)}, u32[]{:S(2)}) %collective-permute-start.7) | collective-permute-done | bytes 131104 | tf_op jit(solution)/shard_map/ppermute | solution.py:23
  36.3 1.7 %shard_map.153 = bf16[512,512]{1,0:T(8,128)(2,1)S(1)} custom-call(s32[44]{0:T(128)S(1)} %get-tuple-element.50.plan, s32[1]{0:T(128)} %bitcast.2.flag, bf16[128,512]{1,0:T(8,128)(2,1)S(1)} %collective-permute-done.4.refs_0_, bf16[128,512]{1,0:T(8,128)(2,1)S(1)} %collective-permute-done.5.refs_1_, bf16[128,512]{1,0:T(8,128)(2,1)S(1)} %collective-permute-done.6.refs_2_, ...), custom_call_target="tpu_custom_call" | custom-call | flops 536870912 | bytes 6291456 | tf_op jit(solution)/shard_map/pallas_call | solution.py:59
  38.0 0.3 collective-permute-start.8
  38.3 1.4 %collective-permute-start.13 = (bf16[512,512]{1,0:T(8,128)(2,1)S(1)}, bf16[512,512]{1,0:T(8,128)(2,1)S(1)}, u32[]{:S(2)}, u32[]{:S(2)}) collective-permute-start(bf16[512,512]{1,0:T(8,128)(2,1)S(1)} %get-tuple-element.78), channel_id=1, source_target_pairs={{24,0},{0,8},{8,16},{16,24},{25,1},{1,9},{9,17},{17,25},{26,2},{2,... | collective-permute-start | bytes 1572872 | tf_op jit(solution)/shard_map/ppermute | solution.py:23
  39.6 7.0 %collective-permute-done.8.nodes.front.refs_6_ = bf16[512,512]{1,0:T(8,128)(2,1)S(1)} collective-permute-done((bf16[512,512]{1,0:T(8,128)(2,1)S(1)}, bf16[512,512]{1,0:T(8,128)(2,1)S(1)}, u32[]{:S(2)}, u32[]{:S(2)}) %collective-permute-start.8) | collective-permute-done | bytes 524320 | tf_op jit(solution)/shard_map/ppermute | solution.py:23
  46.7 0.6 shard_map.154
  47.3 1.9 %collective-permute-start.9 = (bf16[128,512]{1,0:T(8,128)(2,1)S(1)}, bf16[128,512]{1,0:T(8,128)(2,1)S(1)}, u32[]{:S(2)}, u32[]{:S(2)}) collective-permute-start(bf16[128,512]{1,0:T(8,128)(2,1)S(1)} %get-tuple-element.74), channel_id=1, source_target_pairs={{7,0},{0,1},{1,2},{2,3},{3,4},{4,5},{5,6},{6,7},{15,8},{8,9},{9,10... | collective-permute-start | bytes 393224 | tf_op jit(solution)/shard_map/ppermute | solution.py:23
  49.1 0.3 collective-permute-start.10
  49.5 0.0 collective-permute-done.15.edges.refs_11_
  49.5 1.3 %collective-permute-start.11 = (bf16[128,512]{1,0:T(8,128)(2,1)S(1)}, bf16[128,512]{1,0:T(8,128)(2,1)S(1)}, u32[]{:S(2)}, u32[]{:S(2)}) collective-permute-start(bf16[128,512]{1,0:T(8,128)(2,1)S(1)} %get-tuple-element.76), channel_id=1, source_target_pairs={{6,0},{7,1},{0,2},{1,3},{2,4},{3,5},{4,6},{5,7},{14,8},{15,9},{8,1... | collective-permute-start | bytes 393224 | tf_op jit(solution)/shard_map/ppermute | solution.py:23
  50.7 0.6 shard_map.156.refs_5_
  51.3 1.0 %collective-permute-done.13.back = bf16[512,512]{1,0:T(8,128)(2,1)S(1)} collective-permute-done((bf16[512,512]{1,0:T(8,128)(2,1)S(1)}, bf16[512,512]{1,0:T(8,128)(2,1)S(1)}, u32[]{:S(2)}, u32[]{:S(2)}) %collective-permute-start.13) | collective-permute-done | bytes 524320 | tf_op jit(solution)/shard_map/ppermute | solution.py:23
  52.3 4.0 %collective-permute-start.12 = (bf16[128,512]{1,0:T(8,128)(2,1)S(1)}, bf16[128,512]{1,0:T(8,128)(2,1)S(1)}, u32[]{:S(2)}, u32[]{:S(2)}) collective-permute-start(bf16[128,512]{1,0:T(8,128)(2,1)S(1)} %get-tuple-element.77), channel_id=1, source_target_pairs={{2,0},{3,1},{4,2},{5,3},{6,4},{7,5},{0,6},{1,7},{10,8},{11,9},{12,... | collective-permute-start | bytes 393224 | tf_op jit(solution)/shard_map/ppermute | solution.py:23
  56.3 0.0 collective-permute-done.14.edges_one.refs_10_
  56.3 1.7 %shard_map.155 = (f32[768,512]{1,0:T(8,128)S(1)}, bf16[1024,512]{1,0:T(8,128)(2,1)S(1)}, bf16[1024,512]{1,0:T(8,128)(2,1)S(1)}) custom-call(bf16[512,512]{1,0:T(8,128)(2,1)S(1)} %collective-permute-done.8.nodes.front.refs_6_, bf16[512,512]{1,0:T(8,128)(2,1)S(1)} %collective-permute-done.13.back, ...), custom_call_target="tpu_custom_call" | custom-call | flops 1476395008 | bytes 8388608 | tf_op jit(solution)/shard_map/pallas_call | solution.py:59
  58.0 0.0 collective-permute-done.9.refs_0_
  58.0 0.0 collective-permute-done.10.refs_1_
  58.0 0.4 collective-permute-done.11.refs_2_
  58.4 1.4 %collective-permute-done.12.refs_3_ = bf16[128,512]{1,0:T(8,128)(2,1)S(1)} collective-permute-done((bf16[128,512]{1,0:T(8,128)(2,1)S(1)}, bf16[128,512]{1,0:T(8,128)(2,1)S(1)}, u32[]{:S(2)}, u32[]{:S(2)}) %collective-permute-start.12) | collective-permute-done | bytes 131104 | tf_op jit(solution)/shard_map/ppermute | solution.py:23
  59.8 4.8 %shard_map.157 = (bf16[768,512]{1,0:T(8,128)(2,1)S(1)}, bf16[768,512]{1,0:T(8,128)(2,1)S(1)}, bf16[1536,512]{1,0:T(8,128)(2,1)S(1)}, f32[1536,512]{1,0:T(8,128)S...) custom-call(s32[44]{0:T(128)S(1)} %get-tuple-element.50.plan, ...), custom_call_target="tpu_custom_call" | custom-call | flops 1610612736 | bytes 16777216 | tf_op jit(solution)/shard_map/pallas_call | solution.py:59
  64.6 1.8 %collective-permute-start.16 = (bf16[128,512]{1,0:T(8,128)(2,1)S(1)}, bf16[128,512]{1,0:T(8,128)(2,1)S(1)}, u32[]{:S(2)}, u32[]{:S(2)}) collective-permute-start(bf16[128,512]{1,0:T(8,128)(2,1)S(1)} %get-tuple-element.86), channel_id=1, source_target_pairs={{1,0},{2,1},{3,2},{4,3},{5,4},{6,5},{7,6},{0,7},{9,8},{10,9},{11,1... | collective-permute-start | bytes 393224 | tf_op jit(solution)/shard_map/ppermute | solution.py:23
  66.4 1.2 %collective-permute-start.17 = (bf16[128,512]{1,0:T(8,128)(2,1)S(1)}, bf16[128,512]{1,0:T(8,128)(2,1)S(1)}, u32[]{:S(2)}, u32[]{:S(2)}) collective-permute-start(bf16[128,512]{1,0:T(8,128)(2,1)S(1)} %get-tuple-element.87), channel_id=1, source_target_pairs={{7,0},{0,1},{1,2},{2,3},{3,4},{4,5},{5,6},{6,7},{15,8},{8,9},{9,10... | collective-permute-start | bytes 393224 | tf_op jit(solution)/shard_map/ppermute | solution.py:23
  67.6 5.1 %collective-permute-start.18 = (bf16[128,512]{1,0:T(8,128)(2,1)S(1)}, bf16[128,512]{1,0:T(8,128)(2,1)S(1)}, u32[]{:S(2)}, u32[]{:S(2)}) collective-permute-start(bf16[128,512]{1,0:T(8,128)(2,1)S(1)} %get-tuple-element.88), channel_id=1, source_target_pairs={{2,0},{3,1},{4,2},{5,3},{6,4},{7,5},{0,6},{1,7},{10,8},{11,9},{12,... | collective-permute-start | bytes 393224 | tf_op jit(solution)/shard_map/ppermute | solution.py:23
  72.6 0.0 collective-permute-start.19
  72.6 3.5 %shard_map.158 = (f32[512,512]{1,0:T(8,128)S(1)}, f32[512,512]{1,0:T(8,128)S(1)}, bf16[1024,512]{1,0:T(8,128)(2,1)}, bf16[1536,512]{1,0:T(8,128)(2,1)}) custom-call(s32[44]{0:T(128)S(1)} %get-tuple-element.50.plan, bf16[1536,512]{1,0:T(8,128)(2,1)S(1)} %get-tuple-element.90.low, bf16[3072,128]{1,0:T(8,128)(2,1)S(1)} %get-tuple-element.62.refs_9_.flipped, ...), custom_call_target="tpu_custom_call" | custom-call | flops 1073741824 | bytes 12582912 | tf_op jit(solution)/shard_map/pallas_call | solution.py:59
  76.2 0.0 collective-permute-done.16.refs_0_
  76.2 0.0 collective-permute-done.17.refs_1_
  76.2 0.3 collective-permute-done.18.refs_2_
  76.5 2.9 %collective-permute-done.19.refs_3_ = bf16[128,512]{1,0:T(8,128)(2,1)S(1)} collective-permute-done((bf16[128,512]{1,0:T(8,128)(2,1)S(1)}, bf16[128,512]{1,0:T(8,128)(2,1)S(1)}, u32[]{:S(2)}, u32[]{:S(2)}) %collective-permute-start.19) | collective-permute-done | bytes 131104 | tf_op jit(solution)/shard_map/ppermute | solution.py:23
  79.4 2.5 %shard_map.159 = bf16[1024,512]{1,0:T(8,128)(2,1)} custom-call(s32[44]{0:T(128)S(1)} %get-tuple-element.50.plan, bf16[128,512]{1,0:T(8,128)(2,1)S(1)} %collective-permute-done.16.refs_0_, bf16[128,512]{1,0:T(8,128)(2,1)S(1)} %collective-permute-done.17.refs_1_, ...), custom_call_target="tpu_custom_call", output_to_operand_aliasing={{}: (11, {})} | custom-call | flops 536870912 | bytes 6291456 | tf_op jit(solution)/shard_map/pallas_call | solution.py:59
Async XLA Ops:
  2.5 9.9 %collective-permute-start = (bf16[128,512]{1,0:T(8,128)(2,1)S(1)}, bf16[128,512]{1,0:T(8,128)(2,1)S(1)}, u32[]{:S(2)}, u32[]{:S(2)}) collective-permute-start(bf16[128,512]{1,0:T(8,128)(2,1)S(1)} %get-tuple-element.51), channel_id=1, source_target_pairs={{7,0},{0,1},{1,2},{2,3},{3,4},{4,5},{5,6},{6,7},{15,8},{8,9},{9,10... | collective-permute-start | bytes 393224 | tf_op jit(solution)/shard_map/ppermute | solution.py:23
  4.1 8.4 %collective-permute-start.1 = (bf16[128,512]{1,0:T(8,128)(2,1)S(1)}, bf16[128,512]{1,0:T(8,128)(2,1)S(1)}, u32[]{:S(2)}, u32[]{:S(2)}) collective-permute-start(bf16[128,512]{1,0:T(8,128)(2,1)S(1)} %get-tuple-element.52), channel_id=1, source_target_pairs={{1,0},{2,1},{3,2},{4,3},{5,4},{6,5},{7,6},{0,7},{9,8},{10,9},{11,1... | collective-permute-start | bytes 393224 | tf_op jit(solution)/shard_map/ppermute | solution.py:23
  4.6 8.9 %collective-permute-start.2 = (bf16[128,512]{1,0:T(8,128)(2,1)S(1)}, bf16[128,512]{1,0:T(8,128)(2,1)S(1)}, u32[]{:S(2)}, u32[]{:S(2)}) collective-permute-start(bf16[128,512]{1,0:T(8,128)(2,1)S(1)} %get-tuple-element.53), channel_id=1, source_target_pairs={{6,0},{7,1},{0,2},{1,3},{2,4},{3,5},{4,6},{5,7},{14,8},{15,9},{8,1... | collective-permute-start | bytes 393224 | tf_op jit(solution)/shard_map/ppermute | solution.py:23
  6.1 9.1 %collective-permute-start.3 = (bf16[128,512]{1,0:T(8,128)(2,1)S(1)}, bf16[128,512]{1,0:T(8,128)(2,1)S(1)}, u32[]{:S(2)}, u32[]{:S(2)}) collective-permute-start(bf16[128,512]{1,0:T(8,128)(2,1)S(1)} %get-tuple-element.54), channel_id=1, source_target_pairs={{2,0},{3,1},{4,2},{5,3},{6,4},{7,5},{0,6},{1,7},{10,8},{11,9},{12,... | collective-permute-start | bytes 393224 | tf_op jit(solution)/shard_map/ppermute | solution.py:23
  8.4 6.9 %copy-start.2 = (bf16[1,512,512]{2,1,0:T(8,128)(2,1)S(1)}, bf16[1,512,512]{2,1,0:T(8,128)(2,1)}, u32[]{:S(2)}) copy-start(bf16[1,512,512]{2,1,0:T(8,128)(2,1)} %param.19) | copy-start | bytes 1572868
  8.4 6.9 %copy-start.4 = (f32[1,512]{1,0:T(1,128)S(1)}, f32[1,512]{1,0:T(1,128)}, u32[]{:S(2)}) copy-start(f32[1,512]{1,0:T(1,128)} %refs_14_.3) | copy-start | bytes 6148
  15.3 12.6 %copy-start = (bf16[1,1024,512]{2,1,0:T(8,128)(2,1)S(1)}, bf16[1,1024,512]{2,1,0:T(8,128)(2,1)}, u32[]{:S(2)}) copy-start(bf16[1,1024,512]{2,1,0:T(8,128)(2,1)} %param.21) | copy-start | bytes 3145732
  15.3 12.6 %copy-start.1 = (bf16[1,512,512]{2,1,0:T(8,128)(2,1)S(1)}, bf16[1,512,512]{2,1,0:T(8,128)(2,1)}, u32[]{:S(2)}) copy-start(bf16[1,512,512]{2,1,0:T(8,128)(2,1)} %param.22) | copy-start | bytes 1572868
  15.3 12.6 %copy-start.3 = (f32[1,512]{1,0:T(1,128)S(1)}, f32[1,512]{1,0:T(1,128)}, u32[]{:S(2)}) copy-start(f32[1,512]{1,0:T(1,128)} %refs_9_.3) | copy-start | bytes 6148
  20.1 7.2 %collective-permute-start.4 = (bf16[128,512]{1,0:T(8,128)(2,1)S(1)}, bf16[128,512]{1,0:T(8,128)(2,1)S(1)}, u32[]{:S(2)}, u32[]{:S(2)}) collective-permute-start(bf16[128,512]{1,0:T(8,128)(2,1)S(1)} %get-tuple-element.66), channel_id=1, source_target_pairs={{1,0},{2,1},{3,2},{4,3},{5,4},{6,5},{7,6},{0,7},{9,8},{10,9},{11,1... | collective-permute-start | bytes 393224 | tf_op jit(solution)/shard_map/ppermute | solution.py:23
  21.2 28.3 %collective-permute-start.15 = (bf16[768,512]{1,0:T(8,128)(2,1)S(1)}, bf16[768,512]{1,0:T(8,128)(2,1)S(1)}, u32[]{:S(2)}, u32[]{:S(2)}) collective-permute-start(bf16[768,512]{1,0:T(8,128)(2,1)S(1)} %get-tuple-element.83), channel_id=1, source_target_pairs={{24,0},{0,8},{8,16},{16,24},{25,1},{1,9},{9,17},{17,25},{26,2},{2,... | collective-permute-start | bytes 2359304 | tf_op jit(solution)/shard_map/ppermute | solution.py:23
  21.3 35.0 %collective-permute-start.14 = (bf16[768,512]{1,0:T(8,128)(2,1)S(1)}, bf16[768,512]{1,0:T(8,128)(2,1)S(1)}, u32[]{:S(2)}, u32[]{:S(2)}) collective-permute-start(bf16[768,512]{1,0:T(8,128)(2,1)S(1)} %get-tuple-element.79), channel_id=1, source_target_pairs={{24,0},{0,8},{8,16},{16,24},{25,1},{1,9},{9,17},{17,25},{26,2},{2,... | collective-permute-start | bytes 2359304 | tf_op jit(solution)/shard_map/ppermute | solution.py:23
  21.9 8.7 %collective-permute-start.5 = (bf16[128,512]{1,0:T(8,128)(2,1)S(1)}, bf16[128,512]{1,0:T(8,128)(2,1)S(1)}, u32[]{:S(2)}, u32[]{:S(2)}) collective-permute-start(bf16[128,512]{1,0:T(8,128)(2,1)S(1)} %get-tuple-element.67), channel_id=1, source_target_pairs={{7,0},{0,1},{1,2},{2,3},{3,4},{4,5},{5,6},{6,7},{15,8},{8,9},{9,10... | collective-permute-start | bytes 393224 | tf_op jit(solution)/shard_map/ppermute | solution.py:23
  23.9 7.9 %collective-permute-start.6 = (bf16[128,512]{1,0:T(8,128)(2,1)S(1)}, bf16[128,512]{1,0:T(8,128)(2,1)S(1)}, u32[]{:S(2)}, u32[]{:S(2)}) collective-permute-start(bf16[128,512]{1,0:T(8,128)(2,1)S(1)} %get-tuple-element.68), channel_id=1, source_target_pairs={{2,0},{3,1},{4,2},{5,3},{6,4},{7,5},{0,6},{1,7},{10,8},{11,9},{12,... | collective-permute-start | bytes 393224 | tf_op jit(solution)/shard_map/ppermute | solution.py:23
  27.3 9.0 %collective-permute-start.7 = (bf16[128,512]{1,0:T(8,128)(2,1)S(1)}, bf16[128,512]{1,0:T(8,128)(2,1)S(1)}, u32[]{:S(2)}, u32[]{:S(2)}) collective-permute-start(bf16[128,512]{1,0:T(8,128)(2,1)S(1)} %get-tuple-element.69), channel_id=1, source_target_pairs={{6,0},{7,1},{0,2},{1,3},{2,4},{3,5},{4,6},{5,7},{14,8},{15,9},{8,1... | collective-permute-start | bytes 393224 | tf_op jit(solution)/shard_map/ppermute | solution.py:23
  38.0 8.7 %collective-permute-start.8 = (bf16[512,512]{1,0:T(8,128)(2,1)S(1)}, bf16[512,512]{1,0:T(8,128)(2,1)S(1)}, u32[]{:S(2)}, u32[]{:S(2)}) collective-permute-start(bf16[512,512]{1,0:T(8,128)(2,1)S(1)} %shard_map.153), channel_id=1, source_target_pairs={{24,0},{0,8},{8,16},{16,24},{25,1},{1,9},{9,17},{17,25},{26,2},{2,... | collective-permute-start | bytes 1572872 | tf_op jit(solution)/shard_map/ppermute | solution.py:23
  38.3 14.0 %collective-permute-start.13 = (bf16[512,512]{1,0:T(8,128)(2,1)S(1)}, bf16[512,512]{1,0:T(8,128)(2,1)S(1)}, u32[]{:S(2)}, u32[]{:S(2)}) collective-permute-start(bf16[512,512]{1,0:T(8,128)(2,1)S(1)} %get-tuple-element.78), channel_id=1, source_target_pairs={{24,0},{0,8},{8,16},{16,24},{25,1},{1,9},{9,17},{17,25},{26,2},{2,... | collective-permute-start | bytes 1572872 | tf_op jit(solution)/shard_map/ppermute | solution.py:23
  47.3 10.7 %collective-permute-start.9 = (bf16[128,512]{1,0:T(8,128)(2,1)S(1)}, bf16[128,512]{1,0:T(8,128)(2,1)S(1)}, u32[]{:S(2)}, u32[]{:S(2)}) collective-permute-start(bf16[128,512]{1,0:T(8,128)(2,1)S(1)} %get-tuple-element.74), channel_id=1, source_target_pairs={{7,0},{0,1},{1,2},{2,3},{3,4},{4,5},{5,6},{6,7},{15,8},{8,9},{9,10... | collective-permute-start | bytes 393224 | tf_op jit(solution)/shard_map/ppermute | solution.py:23
  49.1 8.8 %collective-permute-start.10 = (bf16[128,512]{1,0:T(8,128)(2,1)S(1)}, bf16[128,512]{1,0:T(8,128)(2,1)S(1)}, u32[]{:S(2)}, u32[]{:S(2)}) collective-permute-start(bf16[128,512]{1,0:T(8,128)(2,1)S(1)} %get-tuple-element.75), channel_id=1, source_target_pairs={{1,0},{2,1},{3,2},{4,3},{5,4},{6,5},{7,6},{0,7},{9,8},{10,9},{11,1... | collective-permute-start | bytes 393224 | tf_op jit(solution)/shard_map/ppermute | solution.py:23
  49.5 8.9 %collective-permute-start.11 = (bf16[128,512]{1,0:T(8,128)(2,1)S(1)}, bf16[128,512]{1,0:T(8,128)(2,1)S(1)}, u32[]{:S(2)}, u32[]{:S(2)}) collective-permute-start(bf16[128,512]{1,0:T(8,128)(2,1)S(1)} %get-tuple-element.76), channel_id=1, source_target_pairs={{6,0},{7,1},{0,2},{1,3},{2,4},{3,5},{4,6},{5,7},{14,8},{15,9},{8,1... | collective-permute-start | bytes 393224 | tf_op jit(solution)/shard_map/ppermute | solution.py:23
  52.3 7.5 %collective-permute-start.12 = (bf16[128,512]{1,0:T(8,128)(2,1)S(1)}, bf16[128,512]{1,0:T(8,128)(2,1)S(1)}, u32[]{:S(2)}, u32[]{:S(2)}) collective-permute-start(bf16[128,512]{1,0:T(8,128)(2,1)S(1)} %get-tuple-element.77), channel_id=1, source_target_pairs={{2,0},{3,1},{4,2},{5,3},{6,4},{7,5},{0,6},{1,7},{10,8},{11,9},{12,... | collective-permute-start | bytes 393224 | tf_op jit(solution)/shard_map/ppermute | solution.py:23
  64.6 11.6 %collective-permute-start.16 = (bf16[128,512]{1,0:T(8,128)(2,1)S(1)}, bf16[128,512]{1,0:T(8,128)(2,1)S(1)}, u32[]{:S(2)}, u32[]{:S(2)}) collective-permute-start(bf16[128,512]{1,0:T(8,128)(2,1)S(1)} %get-tuple-element.86), channel_id=1, source_target_pairs={{1,0},{2,1},{3,2},{4,3},{5,4},{6,5},{7,6},{0,7},{9,8},{10,9},{11,1... | collective-permute-start | bytes 393224 | tf_op jit(solution)/shard_map/ppermute | solution.py:23
  66.4 9.8 %collective-permute-start.17 = (bf16[128,512]{1,0:T(8,128)(2,1)S(1)}, bf16[128,512]{1,0:T(8,128)(2,1)S(1)}, u32[]{:S(2)}, u32[]{:S(2)}) collective-permute-start(bf16[128,512]{1,0:T(8,128)(2,1)S(1)} %get-tuple-element.87), channel_id=1, source_target_pairs={{7,0},{0,1},{1,2},{2,3},{3,4},{4,5},{5,6},{6,7},{15,8},{8,9},{9,10... | collective-permute-start | bytes 393224 | tf_op jit(solution)/shard_map/ppermute | solution.py:23
  67.6 8.9 %collective-permute-start.18 = (bf16[128,512]{1,0:T(8,128)(2,1)S(1)}, bf16[128,512]{1,0:T(8,128)(2,1)S(1)}, u32[]{:S(2)}, u32[]{:S(2)}) collective-permute-start(bf16[128,512]{1,0:T(8,128)(2,1)S(1)} %get-tuple-element.88), channel_id=1, source_target_pairs={{2,0},{3,1},{4,2},{5,3},{6,4},{7,5},{0,6},{1,7},{10,8},{11,9},{12,... | collective-permute-start | bytes 393224 | tf_op jit(solution)/shard_map/ppermute | solution.py:23
  72.6 6.8 %collective-permute-start.19 = (bf16[128,512]{1,0:T(8,128)(2,1)S(1)}, bf16[128,512]{1,0:T(8,128)(2,1)S(1)}, u32[]{:S(2)}, u32[]{:S(2)}) collective-permute-start(bf16[128,512]{1,0:T(8,128)(2,1)S(1)} %get-tuple-element.89), channel_id=1, source_target_pairs={{6,0},{7,1},{0,2},{1,3},{2,4},{3,5},{4,6},{5,7},{14,8},{15,9},{8,1... | collective-permute-start | bytes 393224 | tf_op jit(solution)/shard_map/ppermute | solution.py:23
where the time goes:
time: 83.3 us; the launch traced here: 82.1 us
  starting transfers between devices  30.8 us (37%)
  Pallas kernels  28.6 us (34%)
  waiting for transfers between devices  21.7 us (26%)
  between operations  0.95 us (1%)
    ppermute x20, starting transfers between devices, rotated(): return lax.ppermute(block, axis, route)  30.8 us
    pallas_call x11, Pallas kernels, call(): return step(*values)  28.6 us
    ppermute x20, waiting for transfers between devices, rotated(): return lax.ppermute(block, axis, route)  21.7 us
  transfers between devices with their start and end apart: 20, of which 11 were waited for; matrix products, arithmetic and copies ran while one was open for 0% of the time, Pallas kernels for 18%

commit v1 on v0

--- a/solution.py
+++ b/solution.py
@@ -6,8 +6,8 @@
 from jax.sharding import PartitionSpec as P
 
 
-partner_offsets = (1, -1, 2, -2)
-partners = len(partner_offsets)
+exchanges = ((1, 1), (2, 0), (2, 1), (1, 0))
+partners = len(exchanges)
 epsilon = 1e-05
 f32 = jnp.float32
 bf16 = jnp.bfloat16
@@ -17,10 +17,18 @@
 group = 3
 
 
-def rotated(block, axis, distance):
-    devices = range(lax.axis_size(axis))
-    route = [((i - distance) % len(devices), i) for i in devices]
-    return lax.ppermute(block, axis, route)
+def passed_along(block, axis, distance):
+    count = lax.axis_size(axis)
+    return lax.ppermute(block, axis, [(i, (i + distance) % count) for i in range(count)])
+
+
+def swapped(block, step, phase):
+    count = lax.axis_size("dom")
+    assert count % (2 * step) == 0
+    route = [
+        (i, (i + (step if (i // step) % 2 == phase else -step)) % count) for i in range(count)
+    ]
+    return lax.ppermute(block, "dom", route)
 
 
 def layer_norm(values, gain):
@@ -78,18 +86,27 @@
     return pl.ds(pl.multiple_of(index * rows, rows), rows)
 
 
+def halves(whole, one):
+    rows = one.shape[0]
+    return whole.at[pl.ds(0, rows), :], whole.at[pl.ds(rows, whole.shape[0] - rows), :]
+
+
 def span(index, rows):
     return pl.ds(index * rows, rows)
 
 
-def plan_kernel(sends_far, pairs_far, nodes, plan, front, back, *rest):
+def plan_kernel(place_here, sends_far, pairs_far, nodes, plan, front, back, *rest):
     outs, (near, sends, pairs, sems) = rest[:partners], rest[partners:]
     rows = outs[0].shape[0]
     blocks = nodes.shape[0] // rows
     number = pairs.shape[2]
     copies = started([(sends_far, sends), (nodes, near), (pairs_far, pairs)], sems)
     copies[0].wait()
-    chosen = [sends[0, i] for i in range(partners)]
+    chosen, ahead_of = [], []
+    for step, phase in exchanges:
+        ahead_of.append(lax.rem(place_here[0] // step, 2) == phase)
+        slot = 2 * (step - 1)
+        chosen.append(jnp.where(ahead_of[-1], sends[0, slot], sends[0, slot + 1]))
     used = []
     for block in range(blocks):
         hit = chosen[0] == block
@@ -110,7 +127,11 @@
     for k in range(number):
         code = pairs[1, 0, k]
         local = plan[blocks + pairs[2, 0, k]]
-        plan[2 * blocks + partners + k] = jnp.where(code == 0, local, blocks + code - 1)
+        source = local
+        for i, (step, _) in enumerate(exchanges):
+            arrives = 2 * (step - 1) + 1 + ahead_of[i].astype(jnp.int32)
+            source = jnp.where(code == arrives, blocks + i, source)
+        plan[2 * blocks + partners + k] = source
         plan[2 * blocks + partners + number + k] = plan[blocks + pairs[0, 0, k]]
     copies[1].wait()
     for index, out in zip(chosen, outs):
@@ -152,14 +173,14 @@
 ):
     rows = senders.shape[1]
     width = front.shape[1]
-    half = edges_one.shape[0]
+    near_one, near_two = halves(edges, edges_one)
     copies = started(
         [
             (first.at[span(1, width), :], w_sent),
             (first.at[span(2, width), :], w_received),
             (first.at[span(0, width), :], w_edge),
-            (edges.at[span(0, half), :], edges_one),
-            (edges.at[span(1, half), :], edges_two),
+            (near_one, edges_one),
+            (near_two, edges_two),
             (senders, near_senders),
             (receivers, near_receivers),
         ],
@@ -193,14 +214,11 @@
 
 def edge_kernel(plan, flag, entering, *refs):
     edge_part(plan, refs[:-1])
-    new_edges = refs[partners + 11 : partners + 13]
-    half = new_edges[0].shape[0]
+    one, two = refs[partners + 11 : partners + 13]
 
     @pl.when(flag[0] == 1)
     def _():
-        finish(
-            started([(entering.at[span(i, half), :], new_edges[i]) for i in range(2)], refs[-1])
-        )
+        finish(started(zip(halves(entering, one), (one, two)), refs[-1]))
 
 
 def edge_last_kernel(plan, *refs):
@@ -219,17 +237,18 @@
     (lookup,) = refs[15 + partners :]
     rows = incoming[0].shape[0]
     blocks = sent.shape[0] // rows
-    half = edges[0].shape[0]
-    number = 2 * half // rows
+    number = low.shape[0] // rows
+    each = edges[0].shape[0] // rows
     sources = 2 * blocks + partners
     lookup[: blocks * rows, :] = sent[...]
     for i, block in enumerate(incoming):
         lookup[span(blocks + i, rows), :] = product(block[...], w_sent[...]).astype(bf16)
     sums[...] = jnp.zeros_like(sums)
-    each = half // rows
-    step = group if each % group == 0 else 1
-    for start in range(0, number, step):
-        part, begin = divmod(start, each)
+    step = group if each % group == 0 and number % group == 0 else 1
+    starts = list(range(0, number, step))
+
+    def opened(start):
+        part = int(start >= each)
         hidden = []
         for block in range(start, start + step):
             both = jnp.concatenate(
@@ -243,7 +262,12 @@
                 ends[span(block, rows), :], both
             )
             hidden.append(jnp.maximum(summed, 0.0).astype(bf16))
-        message = layer_norm(product(jnp.concatenate(hidden, axis=0), second[...]), gain[...])
+        return product(jnp.concatenate(hidden, axis=0), second[...])
+
+    def closed(start, raw):
+        part = int(start >= each)
+        begin = start - part * each
+        message = layer_norm(raw, gain[...])
         here = pl.ds(begin * rows, step * rows)
         new_edges[part][here, :] = (edges[part][here, :].astype(f32) + message).astype(bf16)
         rounded = message.astype(bf16)
@@ -254,6 +278,12 @@
                 flipped[span(2 * block, rows), :], rounded[i * rows : (i + 1) * rows, :]
             )
             sums[aligned(plan[sources + block], rows), :] += spread
+
+    raw = opened(starts[0])
+    for now, later in zip(starts, starts[1:] + [None]):
+        ahead = None if later is None else opened(later)
+        closed(now, raw)
+        raw = ahead
     for i, out in enumerate(outs):
         out[...] = sums[span(blocks + i, rows), :].astype(bf16)
 
@@ -318,15 +348,9 @@
     final_nodes, final_edges, total, near, sems,
 ):
     rows = flipped.shape[1]
-    half = edges_one.shape[0]
+    far_one, far_two = halves(final_edges, edges_one)
     blocks = (front.shape[0] + back.shape[0]) // rows
-    copies = started(
-        [
-            (edges_one, final_edges.at[span(0, half), :]),
-            (edges_two, final_edges.at[span(1, half), :]),
-        ],
-        sems,
-    )
+    copies = started([(edges_one, far_one), (edges_two, far_two)], sems)
     near[...] = settle(
         plan, low, flipped, sums, front, back, first, second, gain, own, ready, total
     )
@@ -408,19 +432,23 @@
     edge_second, node_first, node_second = edge_second[0], node_first[0], node_second[0]
     last = lax.axis_index("section") == lax.axis_size("section") - 1
     flag = last.astype(jnp.int32).reshape(1)
+    here = lax.axis_index("dom").astype(jnp.int32).reshape(1)
     node_rows, width = entering_nodes.shape
     edge_rows = entering_edges.shape[0]
     rows = senders.shape[1]
     blocks = node_rows // rows
     number = edge_rows // rows
-    half = edge_rows // 2
+    one_rows = number // 2 * rows
+    two_rows = edge_rows - one_rows
     kept, rest = partners * rows, node_rows - partners * rows
     square = 2 * width * width
     block = ("v", shape((rows, width), bf16))
     front_out = ("v", shape((kept, width), bf16))
     back_out = ("v", shape((rest, width), bf16))
-    half_low = ("v", shape((half, width), bf16))
-    half_wide = ("v", shape((half, width), f32))
+    one_low = ("v", shape((one_rows, width), bf16))
+    two_low = ("v", shape((two_rows, width), bf16))
+    one_wide = ("v", shape((one_rows, width), f32))
+    two_wide = ("v", shape((two_rows, width), f32))
     weight = ("v", shape((width, width), bf16))
     all_low = ("v", shape((node_rows, width), bf16))
     slots = ("v", shape((node_rows + kept, width), f32))
@@ -428,7 +456,7 @@
 
     plan, front, back, *picked = call(
         plan_kernel,
-        [("h", send_list), ("h", jnp.transpose(pair_list, (2, 0, 1))), ("h", node_latents[0])],
+        [("s", here), ("h", send_list), ("h", jnp.transpose(pair_list, (2, 0, 1))), ("h", node_latents[0])],
         [("s", shape((2 * blocks + partners + 2 * number,), jnp.int32)), front_out, back_out]
         + [block] * partners,
         scratch=[pltpu.VMEM((node_rows, width), bf16), pltpu.SMEM((1, partners), jnp.int32), pltpu.SMEM((3, 1, number), jnp.int32)],
@@ -437,7 +465,7 @@
     )
 
     def fetched(picked):
-        return [rotated(picked[i], "dom", partner_offsets[i]) for i in range(partners)]
+        return [swapped(picked[i], *exchanges[i]) for i in range(partners)]
 
     def edge_stage(kernel, extra, incoming, base, sent, received, edges):
         new_one, new_two, low, sums, *partials = call(
@@ -446,7 +474,7 @@
             + extra
             + [("v", value) for value in (*incoming, *base, sent, received, ends, flipped)]
             + [("v", value) for value in (*edges, w_sent, edge_second, edge_gain)],
-            [half_low, half_low, ("v", shape((edge_rows, width), bf16)), slots]
+            [one_low, two_low, ("v", shape((edge_rows, width), bf16)), slots]
             + [block] * partners,
             scratch=[pltpu.VMEM((node_rows + kept, width), bf16)],
             copies=2 if extra else 0,
@@ -456,7 +484,7 @@
         return (new_one, new_two), low, sums, partials
 
     def handed_back(partials):
-        return [rotated(partials[i], "dom", -partner_offsets[i]) for i in range(partners)]
+        return [swapped(partials[i], *exchanges[i]) for i in range(partners)]
 
     incoming = fetched(picked)
     (
@@ -475,7 +503,7 @@
         load_kernel,
         [("v", front), ("v", back)]
         + [("h", value) for value in (edge_latents[0], edge_first[0], senders, receivers)],
-        [half_low, half_low, weight, weight, weight, half_wide, half_wide]
+        [one_low, two_low, weight, weight, weight, one_wide, two_wide]
         + [all_low, all_low]
         + [("v", shape((edge_rows, 2 * rows), bf16)), ("v", shape((2 * edge_rows, rows), bf16))],
         scratch=[pltpu.VMEM((edge_rows, rows), jnp.int32)] * 2,
@@ -489,7 +517,7 @@
         incoming,
         (base_one, base_two), sent, received, (edges_one, edges_two)
     )
-    edges_one = rotated(edges[0], "section", 1)
+    edges_one = passed_along(edges[0], "section", 1)
     returned = handed_back(partials)
     own, ready, new_back = call(
         settle_kernel,
@@ -505,7 +533,7 @@
         flops=square * 2 * node_rows,
         moved=12 << 20,
     )
-    back = rotated(new_back, "section", 1)
+    back = passed_along(new_back, "section", 1)
     (new_front,) = call(
         node_kernel,
         [("s", plan), ("s", flag)]
@@ -520,8 +548,8 @@
         flops=square * 2 * kept,
         moved=6 << 20,
     )
-    front = rotated(new_front, "section", 1)
-    edges_two = rotated(edges[1], "section", 1)
+    front = passed_along(new_front, "section", 1)
+    edges_two = passed_along(edges[1], "section", 1)
 
     picked = call(
         lambda plan, nodes, *outs: pick(plan, nodes, outs, blocks),
@@ -533,15 +561,15 @@
     base_one, sent, received = call(
         project_kernel,
         [("v", value) for value in (front, back, edges_one, w_edge, w_sent, w_received)],
-        [half_wide, all_low, all_low],
-        flops=square * (half + 2 * node_rows),
+        [one_wide, all_low, all_low],
+        flops=square * (one_rows + 2 * node_rows),
         moved=8 << 20,
     )
     (base_two,) = call(
         base_kernel,
         [("v", edges_two), ("v", w_edge)],
-        [half_wide],
-        flops=square * half,
+        [two_wide],
+        flops=square * two_rows,
         moved=3 << 20,
     )
     edges, low, sums, partials = edge_stage(

time: 83.3 us -> 78.8 us (0.946)
  the two profiles are of different devices: /device:TPU:6 before, /device:TPU:0 now
where the time goes in v1:
time: 78.8 us; the launch traced here: 78.6 us
  starting transfers between devices  28.5 us (36%)
  Pallas kernels  26.8 us (34%)
  waiting for transfers between devices  22.3 us (28%)
  between operations  0.95 us (1%)
    pallas_call x11, Pallas kernels, call(): return step(*values)  26.8 us
    ppermute x16, starting transfers between devices, swapped(): return lax.ppermute(block, 'dom', route)  24.1 us
    ppermute x16, waiting for transfers between devices, swapped(): return lax.ppermute(block, 'dom', route)  12.3 us
    ppermute x4, waiting for transfers between devices, passed_along(): lax.ppermute(block, axis, [(i, (i + distance) % count) for i in range(cou...  9.98 us
    ppermute x4, starting transfers between devices, passed_along(): lax.ppermute(block, axis, [(i, (i + distance) % count) for i in range(cou...  4.42 us
  transfers between devices with their start and end apart: 20, of which 10 were waited for; matrix products, arithmetic and copies ran while one was open for 0% of the time, Pallas kernels for 19%

profile of v1, /device:TPU:0, one launch (start us, length us, event | category | flops | bytes accessed | tf_op | source)
XLA Modules:
  0.0 78.6 jit_solution(1752295011850491394)
XLA Ops:
  0.6 1.9 %shard_map.149 = (s32[44]{0:T(128)S(1)}, bf16[512,512]{1,0:T(8,128)(2,1)S(1)}, bf16[512,512]{1,0:T(8,128)(2,1)S(1)}, bf16[128,512]{1,0:T(8,128)(2,1)S(1)}, bf16[...) custom-call(s32[1]{0:T(128)} %bitcast.place_here, s32[1,4]{1,0:T(1,128)} %sends_far.1, ...), custom_call_target="tpu_custom_call" | custom-call | bytes 1048576 | tf_op jit(solution)/shard_map/pallas_call | solution.py:67
  2.5 6.1 %collective-permute-start = (bf16[128,512]{1,0:T(8,128)(2,1)S(1)}, bf16[128,512]{1,0:T(8,128)(2,1)S(1)}, u32[]{:S(2)}, u32[]{:S(2)}) collective-permute-start(bf16[128,512]{1,0:T(8,128)(2,1)S(1)} %get-tuple-element.51), channel_id=1, source_target_pairs={{0,7},{1,2},{2,1},{3,4},{4,3},{5,6},{6,5},{7,0},{8,15},{9,10},{10,... | collective-permute-start | bytes 393224 | tf_op jit(solution)/shard_map/ppermute | solution.py:31
  8.6 0.0 collective-permute-start.1
  8.6 0.9 %collective-permute-start.2 = (bf16[128,512]{1,0:T(8,128)(2,1)S(1)}, bf16[128,512]{1,0:T(8,128)(2,1)S(1)}, u32[]{:S(2)}, u32[]{:S(2)}) collective-permute-start(bf16[128,512]{1,0:T(8,128)(2,1)S(1)} %get-tuple-element.53), channel_id=1, source_target_pairs={{0,6},{1,7},{2,4},{3,5},{4,2},{5,3},{6,0},{7,1},{8,14},{9,15},{10,... | collective-permute-start | bytes 393224 | tf_op jit(solution)/shard_map/ppermute | solution.py:31
  9.5 1.6 %collective-permute-start.3 = (bf16[128,512]{1,0:T(8,128)(2,1)S(1)}, bf16[128,512]{1,0:T(8,128)(2,1)S(1)}, u32[]{:S(2)}, u32[]{:S(2)}) collective-permute-start(bf16[128,512]{1,0:T(8,128)(2,1)S(1)} %get-tuple-element.54), channel_id=1, source_target_pairs={{0,1},{1,0},{2,3},{3,2},{4,5},{5,4},{6,7},{7,6},{8,9},{9,8},{10,11... | collective-permute-start | bytes 393224 | tf_op jit(solution)/shard_map/ppermute | solution.py:31
  11.1 0.0 copy-start.2
  11.1 0.0 copy-start.4
  11.1 4.0 %shard_map.150 = (bf16[768,512]{1,0:T(8,128)(2,1)S(1)}, bf16[768,512]{1,0:T(8,128)(2,1)S(1)}, bf16[512,512]{1,0:T(8,128)(2,1)S(1)}, bf16[512,512]{1,0:T(8,128)(2...) custom-call(bf16[512,512]{1,0:T(8,128)(2,1)S(1)} %get-tuple-element., ...), custom_call_target="tpu_custom_call" | custom-call | flops 1879048192 | bytes 16777216 | tf_op jit(solution)/shard_map/pallas_call | solution.py:67
  15.2 0.0 collective-permute-done.refs_0_
  15.2 0.1 collective-permute-done.1.refs_1_
  15.3 2.6 %collective-permute-done.2.refs_2_ = bf16[128,512]{1,0:T(8,128)(2,1)S(1)} collective-permute-done((bf16[128,512]{1,0:T(8,128)(2,1)S(1)}, bf16[128,512]{1,0:T(8,128)(2,1)S(1)}, u32[]{:S(2)}, u32[]{:S(2)}) %collective-permute-start.2) | collective-permute-done | bytes 131104 | tf_op jit(solution)/shard_map/ppermute | solution.py:31
  17.9 0.0 collective-permute-done.3.refs_3_
  17.9 0.0 copy-done.2
  17.9 0.0 copy-done.4
  17.9 0.0 copy-start
  17.9 0.0 copy-start.1
  17.9 0.0 copy-start.3
  17.9 3.9 %shard_map.151 = (bf16[768,512]{1,0:T(8,128)(2,1)S(1)}, bf16[768,512]{1,0:T(8,128)(2,1)S(1)}, bf16[1536,512]{1,0:T(8,128)(2,1)S(1)}, f32[1536,512]{1,0:T(8,128)S...) custom-call(s32[44]{0:T(128)S(1)} %get-tuple-element.50.plan, ...), custom_call_target="tpu_custom_call" | custom-call | flops 1610612736 | bytes 16777216 | tf_op jit(solution)/shard_map/pallas_call | solution.py:67
  21.8 1.6 %collective-permute-start.4 = (bf16[128,512]{1,0:T(8,128)(2,1)S(1)}, bf16[128,512]{1,0:T(8,128)(2,1)S(1)}, u32[]{:S(2)}, u32[]{:S(2)}) collective-permute-start(bf16[128,512]{1,0:T(8,128)(2,1)S(1)} %get-tuple-element.66), channel_id=1, source_target_pairs={{0,7},{1,2},{2,1},{3,4},{4,3},{5,6},{6,5},{7,0},{8,15},{9,10},{10,... | collective-permute-start | bytes 393224 | tf_op jit(solution)/shard_map/ppermute | solution.py:31
  23.4 0.0 collective-permute-start.15
  23.4 1.6 %collective-permute-start.14 = (bf16[768,512]{1,0:T(8,128)(2,1)S(1)}, bf16[768,512]{1,0:T(8,128)(2,1)S(1)}, u32[]{:S(2)}, u32[]{:S(2)}) collective-permute-start(bf16[768,512]{1,0:T(8,128)(2,1)S(1)} %get-tuple-element.79), channel_id=1, source_target_pairs={{0,8},{8,16},{16,24},{24,0},{1,9},{9,17},{17,25},{25,1},{2,10},{10... | collective-permute-start | bytes 2359304 | tf_op jit(solution)/shard_map/ppermute | solution.py:22
  25.0 0.3 collective-permute-start.5
  25.3 1.6 %collective-permute-start.6 = (bf16[128,512]{1,0:T(8,128)(2,1)S(1)}, bf16[128,512]{1,0:T(8,128)(2,1)S(1)}, u32[]{:S(2)}, u32[]{:S(2)}) collective-permute-start(bf16[128,512]{1,0:T(8,128)(2,1)S(1)} %get-tuple-element.68), channel_id=1, source_target_pairs={{0,6},{1,7},{2,4},{3,5},{4,2},{5,3},{6,0},{7,1},{8,14},{9,15},{10,... | collective-permute-start | bytes 393224 | tf_op jit(solution)/shard_map/ppermute | solution.py:31
  26.9 2.7 %collective-permute-done.4.refs_0_ = bf16[128,512]{1,0:T(8,128)(2,1)S(1)} collective-permute-done((bf16[128,512]{1,0:T(8,128)(2,1)S(1)}, bf16[128,512]{1,0:T(8,128)(2,1)S(1)}, u32[]{:S(2)}, u32[]{:S(2)}) %collective-permute-start.4) | collective-permute-done | bytes 131104 | tf_op jit(solution)/shard_map/ppermute | solution.py:31
  29.6 0.7 collective-permute-start.7
  30.3 0.0 copy-done
  30.3 0.0 copy-done.1
  30.3 0.0 copy-done.3
  30.3 2.7 %shard_map.152 = (f32[512,512]{1,0:T(8,128)S(1)}, f32[512,512]{1,0:T(8,128)S(1)}, bf16[512,512]{1,0:T(8,128)(2,1)S(1)}) custom-call(s32[44]{0:T(128)S(1)} %get-tuple-element.50.plan, s32[1]{0:T(128)} %bitcast.3.flag, bf16[1536,512]{1,0:T(8,128)(2,1)S(1)} %get-tuple-element.70.low, bf16[3072,128]{1,0:T(8,128)(2,1)S(1)} %get-tuple-element.62.refs_9_.flipped, ...), custom_call_target="tpu_custom_call" | custom-call | flops 1073741824 | bytes 12582912 | tf_op jit(solution)/shard_map/pallas_call | solution.py:67
  33.0 1.1 %collective-permute-done.5.refs_1_ = bf16[128,512]{1,0:T(8,128)(2,1)S(1)} collective-permute-done((bf16[128,512]{1,0:T(8,128)(2,1)S(1)}, bf16[128,512]{1,0:T(8,128)(2,1)S(1)}, u32[]{:S(2)}, u32[]{:S(2)}) %collective-permute-start.5) | collective-permute-done | bytes 131104 | tf_op jit(solution)/shard_map/ppermute | solution.py:31
  34.1 0.0 collective-permute-done.6.refs_2_
  34.1 0.5 collective-permute-done.7.refs_3_
  34.6 1.7 %shard_map.153 = bf16[512,512]{1,0:T(8,128)(2,1)S(1)} custom-call(s32[44]{0:T(128)S(1)} %get-tuple-element.50.plan, s32[1]{0:T(128)} %bitcast.3.flag, bf16[128,512]{1,0:T(8,128)(2,1)S(1)} %collective-permute-done.4.refs_0_, bf16[128,512]{1,0:T(8,128)(2,1)S(1)} %collective-permute-done.5.refs_1_, bf16[128,512]{1,0:T(8,128)(2,1)S(1)} %collective-permute-done.6.refs_2_, ...), custom_call_target="tpu_custom_call" | custom-call | flops 536870912 | bytes 6291456 | tf_op jit(solution)/shard_map/pallas_call | solution.py:67
  36.3 0.1 collective-permute-start.8
  36.4 2.8 %collective-permute-start.13 = (bf16[512,512]{1,0:T(8,128)(2,1)S(1)}, bf16[512,512]{1,0:T(8,128)(2,1)S(1)}, u32[]{:S(2)}, u32[]{:S(2)}) collective-permute-start(bf16[512,512]{1,0:T(8,128)(2,1)S(1)} %get-tuple-element.78), channel_id=1, source_target_pairs={{0,8},{8,16},{16,24},{24,0},{1,9},{9,17},{17,25},{25,1},{2,10},{10... | collective-permute-start | bytes 1572872 | tf_op jit(solution)/shard_map/ppermute | solution.py:22
  39.1 10.0 %collective-permute-done.8.nodes.front.refs_6_ = bf16[512,512]{1,0:T(8,128)(2,1)S(1)} collective-permute-done((bf16[512,512]{1,0:T(8,128)(2,1)S(1)}, bf16[512,512]{1,0:T(8,128)(2,1)S(1)}, u32[]{:S(2)}, u32[]{:S(2)}) %collective-permute-start.8) | collective-permute-done | bytes 524320 | tf_op jit(solution)/shard_map/ppermute | solution.py:22
  49.1 0.6 shard_map.154
  49.7 3.0 %collective-permute-start.9 = (bf16[128,512]{1,0:T(8,128)(2,1)S(1)}, bf16[128,512]{1,0:T(8,128)(2,1)S(1)}, u32[]{:S(2)}, u32[]{:S(2)}) collective-permute-start(bf16[128,512]{1,0:T(8,128)(2,1)S(1)} %get-tuple-element.74), channel_id=1, source_target_pairs={{0,7},{1,2},{2,1},{3,4},{4,3},{5,6},{6,5},{7,0},{8,15},{9,10},{10,... | collective-permute-start | bytes 393224 | tf_op jit(solution)/shard_map/ppermute | solution.py:31
  52.7 0.0 collective-permute-start.10
  52.7 0.0 collective-permute-done.15.edges.refs_11_
  52.7 1.6 %collective-permute-start.11 = (bf16[128,512]{1,0:T(8,128)(2,1)S(1)}, bf16[128,512]{1,0:T(8,128)(2,1)S(1)}, u32[]{:S(2)}, u32[]{:S(2)}) collective-permute-start(bf16[128,512]{1,0:T(8,128)(2,1)S(1)} %get-tuple-element.76), channel_id=1, source_target_pairs={{0,6},{1,7},{2,4},{3,5},{4,2},{5,3},{6,0},{7,1},{8,14},{9,15},{10,... | collective-permute-start | bytes 393224 | tf_op jit(solution)/shard_map/ppermute | solution.py:31
  54.3 0.6 shard_map.156.refs_5_
  54.9 0.0 collective-permute-done.13.back
  54.9 0.8 %collective-permute-start.12 = (bf16[128,512]{1,0:T(8,128)(2,1)S(1)}, bf16[128,512]{1,0:T(8,128)(2,1)S(1)}, u32[]{:S(2)}, u32[]{:S(2)}) collective-permute-start(bf16[128,512]{1,0:T(8,128)(2,1)S(1)} %get-tuple-element.77), channel_id=1, source_target_pairs={{0,1},{1,0},{2,3},{3,2},{4,5},{5,4},{6,7},{7,6},{8,9},{9,8},{10,11... | collective-permute-start | bytes 393224 | tf_op jit(solution)/shard_map/ppermute | solution.py:31
  55.7 0.0 collective-permute-done.14.edges_one.refs_10_
  55.7 1.7 %shard_map.155 = (f32[768,512]{1,0:T(8,128)S(1)}, bf16[1024,512]{1,0:T(8,128)(2,1)S(1)}, bf16[1024,512]{1,0:T(8,128)(2,1)S(1)}) custom-call(bf16[512,512]{1,0:T(8,128)(2,1)S(1)} %collective-permute-done.8.nodes.front.refs_6_, bf16[512,512]{1,0:T(8,128)(2,1)S(1)} %collective-permute-done.13.back, ...), custom_call_target="tpu_custom_call" | custom-call | flops 1476395008 | bytes 8388608 | tf_op jit(solution)/shard_map/pallas_call | solution.py:67
  57.4 1.6 %collective-permute-done.9.refs_0_ = bf16[128,512]{1,0:T(8,128)(2,1)S(1)} collective-permute-done((bf16[128,512]{1,0:T(8,128)(2,1)S(1)}, bf16[128,512]{1,0:T(8,128)(2,1)S(1)}, u32[]{:S(2)}, u32[]{:S(2)}) %collective-permute-start.9) | collective-permute-done | bytes 131104 | tf_op jit(solution)/shard_map/ppermute | solution.py:31
  58.9 0.0 collective-permute-done.10.refs_1_
  59.0 3.4 %collective-permute-done.11.refs_2_ = bf16[128,512]{1,0:T(8,128)(2,1)S(1)} collective-permute-done((bf16[128,512]{1,0:T(8,128)(2,1)S(1)}, bf16[128,512]{1,0:T(8,128)(2,1)S(1)}, u32[]{:S(2)}, u32[]{:S(2)}) %collective-permute-start.11) | collective-permute-done | bytes 131104 | tf_op jit(solution)/shard_map/ppermute | solution.py:31
  62.4 0.0 collective-permute-done.12.refs_3_
  62.4 3.9 %shard_map.157 = (bf16[768,512]{1,0:T(8,128)(2,1)S(1)}, bf16[768,512]{1,0:T(8,128)(2,1)S(1)}, bf16[1536,512]{1,0:T(8,128)(2,1)S(1)}, f32[1536,512]{1,0:T(8,128)S...) custom-call(s32[44]{0:T(128)S(1)} %get-tuple-element.50.plan, ...), custom_call_target="tpu_custom_call" | custom-call | flops 1610612736 | bytes 16777216 | tf_op jit(solution)/shard_map/pallas_call | solution.py:67
  66.3 1.1 %collective-permute-start.16 = (bf16[128,512]{1,0:T(8,128)(2,1)S(1)}, bf16[128,512]{1,0:T(8,128)(2,1)S(1)}, u32[]{:S(2)}, u32[]{:S(2)}) collective-permute-start(bf16[128,512]{1,0:T(8,128)(2,1)S(1)} %get-tuple-element.86), channel_id=1, source_target_pairs={{0,7},{1,2},{2,1},{3,4},{4,3},{5,6},{6,5},{7,0},{8,15},{9,10},{10,... | collective-permute-start | bytes 393224 | tf_op jit(solution)/shard_map/ppermute | solution.py:31
  67.3 1.0 %collective-permute-start.17 = (bf16[128,512]{1,0:T(8,128)(2,1)S(1)}, bf16[128,512]{1,0:T(8,128)(2,1)S(1)}, u32[]{:S(2)}, u32[]{:S(2)}) collective-permute-start(bf16[128,512]{1,0:T(8,128)(2,1)S(1)} %get-tuple-element.87), channel_id=1, source_target_pairs={{0,2},{1,3},{2,0},{3,1},{4,6},{5,7},{6,4},{7,5},{8,10},{9,11},{10,... | collective-permute-start | bytes 393224 | tf_op jit(solution)/shard_map/ppermute | solution.py:31
  68.4 0.4 collective-permute-start.18
  68.8 3.3 %collective-permute-start.19 = (bf16[128,512]{1,0:T(8,128)(2,1)S(1)}, bf16[128,512]{1,0:T(8,128)(2,1)S(1)}, u32[]{:S(2)}, u32[]{:S(2)}) collective-permute-start(bf16[128,512]{1,0:T(8,128)(2,1)S(1)} %get-tuple-element.89), channel_id=1, source_target_pairs={{0,1},{1,0},{2,3},{3,2},{4,5},{5,4},{6,7},{7,6},{8,9},{9,8},{10,11... | collective-permute-start | bytes 393224 | tf_op jit(solution)/shard_map/ppermute | solution.py:31
  72.1 3.5 %shard_map.158 = (f32[512,512]{1,0:T(8,128)S(1)}, f32[512,512]{1,0:T(8,128)S(1)}, bf16[1024,512]{1,0:T(8,128)(2,1)}, bf16[1536,512]{1,0:T(8,128)(2,1)}) custom-call(s32[44]{0:T(128)S(1)} %get-tuple-element.50.plan, bf16[1536,512]{1,0:T(8,128)(2,1)S(1)} %get-tuple-element.90.low, bf16[3072,128]{1,0:T(8,128)(2,1)S(1)} %get-tuple-element.62.refs_9_.flipped, ...), custom_call_target="tpu_custom_call" | custom-call | flops 1073741824 | bytes 12582912 | tf_op jit(solution)/shard_map/pallas_call | solution.py:67
  75.6 0.0 collective-permute-done.16.refs_0_
  75.6 0.0 collective-permute-done.17.refs_1_
  75.6 0.2 collective-permute-done.18.refs_2_
  75.9 0.1 collective-permute-done.19.refs_3_
  75.9 2.5 %shard_map.159 = bf16[1024,512]{1,0:T(8,128)(2,1)} custom-call(s32[44]{0:T(128)S(1)} %get-tuple-element.50.plan, bf16[128,512]{1,0:T(8,128)(2,1)S(1)} %collective-permute-done.16.refs_0_, bf16[128,512]{1,0:T(8,128)(2,1)S(1)} %collective-permute-done.17.refs_1_, ...), custom_call_target="tpu_custom_call", output_to_operand_aliasing={{}: (11, {})} | custom-call | flops 536870912 | bytes 6291456 | tf_op jit(solution)/shard_map/pallas_call | solution.py:67
Async XLA Ops:
  2.5 12.7 %collective-permute-start = (bf16[128,512]{1,0:T(8,128)(2,1)S(1)}, bf16[128,512]{1,0:T(8,128)(2,1)S(1)}, u32[]{:S(2)}, u32[]{:S(2)}) collective-permute-start(bf16[128,512]{1,0:T(8,128)(2,1)S(1)} %get-tuple-element.51), channel_id=1, source_target_pairs={{0,7},{1,2},{2,1},{3,4},{4,3},{5,6},{6,5},{7,0},{8,15},{9,10},{10,... | collective-permute-start | bytes 393224 | tf_op jit(solution)/shard_map/ppermute | solution.py:31
  8.6 6.7 %collective-permute-start.1 = (bf16[128,512]{1,0:T(8,128)(2,1)S(1)}, bf16[128,512]{1,0:T(8,128)(2,1)S(1)}, u32[]{:S(2)}, u32[]{:S(2)}) collective-permute-start(bf16[128,512]{1,0:T(8,128)(2,1)S(1)} %get-tuple-element.52), channel_id=1, source_target_pairs={{0,2},{1,3},{2,0},{3,1},{4,6},{5,7},{6,4},{7,5},{8,10},{9,11},{10,... | collective-permute-start | bytes 393224 | tf_op jit(solution)/shard_map/ppermute | solution.py:31
  8.6 9.3 %collective-permute-start.2 = (bf16[128,512]{1,0:T(8,128)(2,1)S(1)}, bf16[128,512]{1,0:T(8,128)(2,1)S(1)}, u32[]{:S(2)}, u32[]{:S(2)}) collective-permute-start(bf16[128,512]{1,0:T(8,128)(2,1)S(1)} %get-tuple-element.53), channel_id=1, source_target_pairs={{0,6},{1,7},{2,4},{3,5},{4,2},{5,3},{6,0},{7,1},{8,14},{9,15},{10,... | collective-permute-start | bytes 393224 | tf_op jit(solution)/shard_map/ppermute | solution.py:31
  9.5 8.4 %collective-permute-start.3 = (bf16[128,512]{1,0:T(8,128)(2,1)S(1)}, bf16[128,512]{1,0:T(8,128)(2,1)S(1)}, u32[]{:S(2)}, u32[]{:S(2)}) collective-permute-start(bf16[128,512]{1,0:T(8,128)(2,1)S(1)} %get-tuple-element.54), channel_id=1, source_target_pairs={{0,1},{1,0},{2,3},{3,2},{4,5},{5,4},{6,7},{7,6},{8,9},{9,8},{10,11... | collective-permute-start | bytes 393224 | tf_op jit(solution)/shard_map/ppermute | solution.py:31
  11.1 6.7 %copy-start.2 = (bf16[1,512,512]{2,1,0:T(8,128)(2,1)S(1)}, bf16[1,512,512]{2,1,0:T(8,128)(2,1)}, u32[]{:S(2)}) copy-start(bf16[1,512,512]{2,1,0:T(8,128)(2,1)} %param.19) | copy-start | bytes 1572868
  11.1 6.8 %copy-start.4 = (f32[1,512]{1,0:T(1,128)S(1)}, f32[1,512]{1,0:T(1,128)}, u32[]{:S(2)}) copy-start(f32[1,512]{1,0:T(1,128)} %refs_14_.3) | copy-start | bytes 6148
  17.9 12.5 %copy-start = (bf16[1,1024,512]{2,1,0:T(8,128)(2,1)S(1)}, bf16[1,1024,512]{2,1,0:T(8,128)(2,1)}, u32[]{:S(2)}) copy-start(bf16[1,1024,512]{2,1,0:T(8,128)(2,1)} %param.21) | copy-start | bytes 3145732
  17.9 12.4 %copy-start.1 = (bf16[1,512,512]{2,1,0:T(8,128)(2,1)S(1)}, bf16[1,512,512]{2,1,0:T(8,128)(2,1)}, u32[]{:S(2)}) copy-start(bf16[1,512,512]{2,1,0:T(8,128)(2,1)} %param.22) | copy-start | bytes 1572868
  17.9 12.4 %copy-start.3 = (f32[1,512]{1,0:T(1,128)S(1)}, f32[1,512]{1,0:T(1,128)}, u32[]{:S(2)}) copy-start(f32[1,512]{1,0:T(1,128)} %refs_9_.3) | copy-start | bytes 6148
  21.8 7.8 %collective-permute-start.4 = (bf16[128,512]{1,0:T(8,128)(2,1)S(1)}, bf16[128,512]{1,0:T(8,128)(2,1)S(1)}, u32[]{:S(2)}, u32[]{:S(2)}) collective-permute-start(bf16[128,512]{1,0:T(8,128)(2,1)S(1)} %get-tuple-element.66), channel_id=1, source_target_pairs={{0,7},{1,2},{2,1},{3,4},{4,3},{5,6},{6,5},{7,0},{8,15},{9,10},{10,... | collective-permute-start | bytes 393224 | tf_op jit(solution)/shard_map/ppermute | solution.py:31
  23.4 29.3 %collective-permute-start.15 = (bf16[768,512]{1,0:T(8,128)(2,1)S(1)}, bf16[768,512]{1,0:T(8,128)(2,1)S(1)}, u32[]{:S(2)}, u32[]{:S(2)}) collective-permute-start(bf16[768,512]{1,0:T(8,128)(2,1)S(1)} %get-tuple-element.83), channel_id=1, source_target_pairs={{0,8},{8,16},{16,24},{24,0},{1,9},{9,17},{17,25},{25,1},{2,10},{10... | collective-permute-start | bytes 2359304 | tf_op jit(solution)/shard_map/ppermute | solution.py:22
  23.4 32.3 %collective-permute-start.14 = (bf16[768,512]{1,0:T(8,128)(2,1)S(1)}, bf16[768,512]{1,0:T(8,128)(2,1)S(1)}, u32[]{:S(2)}, u32[]{:S(2)}) collective-permute-start(bf16[768,512]{1,0:T(8,128)(2,1)S(1)} %get-tuple-element.79), channel_id=1, source_target_pairs={{0,8},{8,16},{16,24},{24,0},{1,9},{9,17},{17,25},{25,1},{2,10},{10... | collective-permute-start | bytes 2359304 | tf_op jit(solution)/shard_map/ppermute | solution.py:22
  25.0 9.1 %collective-permute-start.5 = (bf16[128,512]{1,0:T(8,128)(2,1)S(1)}, bf16[128,512]{1,0:T(8,128)(2,1)S(1)}, u32[]{:S(2)}, u32[]{:S(2)}) collective-permute-start(bf16[128,512]{1,0:T(8,128)(2,1)S(1)} %get-tuple-element.67), channel_id=1, source_target_pairs={{0,2},{1,3},{2,0},{3,1},{4,6},{5,7},{6,4},{7,5},{8,10},{9,11},{10,... | collective-permute-start | bytes 393224 | tf_op jit(solution)/shard_map/ppermute | solution.py:31
  25.3 8.8 %collective-permute-start.6 = (bf16[128,512]{1,0:T(8,128)(2,1)S(1)}, bf16[128,512]{1,0:T(8,128)(2,1)S(1)}, u32[]{:S(2)}, u32[]{:S(2)}) collective-permute-start(bf16[128,512]{1,0:T(8,128)(2,1)S(1)} %get-tuple-element.68), channel_id=1, source_target_pairs={{0,6},{1,7},{2,4},{3,5},{4,2},{5,3},{6,0},{7,1},{8,14},{9,15},{10,... | collective-permute-start | bytes 393224 | tf_op jit(solution)/shard_map/ppermute | solution.py:31
  29.6 5.0 %collective-permute-start.7 = (bf16[128,512]{1,0:T(8,128)(2,1)S(1)}, bf16[128,512]{1,0:T(8,128)(2,1)S(1)}, u32[]{:S(2)}, u32[]{:S(2)}) collective-permute-start(bf16[128,512]{1,0:T(8,128)(2,1)S(1)} %get-tuple-element.69), channel_id=1, source_target_pairs={{0,1},{1,0},{2,3},{3,2},{4,5},{5,4},{6,7},{7,6},{8,9},{9,8},{10,11... | collective-permute-start | bytes 393224 | tf_op jit(solution)/shard_map/ppermute | solution.py:31
  36.3 12.8 %collective-permute-start.8 = (bf16[512,512]{1,0:T(8,128)(2,1)S(1)}, bf16[512,512]{1,0:T(8,128)(2,1)S(1)}, u32[]{:S(2)}, u32[]{:S(2)}) collective-permute-start(bf16[512,512]{1,0:T(8,128)(2,1)S(1)} %shard_map.153), channel_id=1, source_target_pairs={{0,8},{8,16},{16,24},{24,0},{1,9},{9,17},{17,25},{25,1},{2,10},{10... | collective-permute-start | bytes 1572872 | tf_op jit(solution)/shard_map/ppermute | solution.py:22
  36.4 18.5 %collective-permute-start.13 = (bf16[512,512]{1,0:T(8,128)(2,1)S(1)}, bf16[512,512]{1,0:T(8,128)(2,1)S(1)}, u32[]{:S(2)}, u32[]{:S(2)}) collective-permute-start(bf16[512,512]{1,0:T(8,128)(2,1)S(1)} %get-tuple-element.78), channel_id=1, source_target_pairs={{0,8},{8,16},{16,24},{24,0},{1,9},{9,17},{17,25},{25,1},{2,10},{10... | collective-permute-start | bytes 1572872 | tf_op jit(solution)/shard_map/ppermute | solution.py:22
  49.7 9.2 %collective-permute-start.9 = (bf16[128,512]{1,0:T(8,128)(2,1)S(1)}, bf16[128,512]{1,0:T(8,128)(2,1)S(1)}, u32[]{:S(2)}, u32[]{:S(2)}) collective-permute-start(bf16[128,512]{1,0:T(8,128)(2,1)S(1)} %get-tuple-element.74), channel_id=1, source_target_pairs={{0,7},{1,2},{2,1},{3,4},{4,3},{5,6},{6,5},{7,0},{8,15},{9,10},{10,... | collective-permute-start | bytes 393224 | tf_op jit(solution)/shard_map/ppermute | solution.py:31
  52.7 6.3 %collective-permute-start.10 = (bf16[128,512]{1,0:T(8,128)(2,1)S(1)}, bf16[128,512]{1,0:T(8,128)(2,1)S(1)}, u32[]{:S(2)}, u32[]{:S(2)}) collective-permute-start(bf16[128,512]{1,0:T(8,128)(2,1)S(1)} %get-tuple-element.75), channel_id=1, source_target_pairs={{0,2},{1,3},{2,0},{3,1},{4,6},{5,7},{6,4},{7,5},{8,10},{9,11},{10,... | collective-permute-start | bytes 393224 | tf_op jit(solution)/shard_map/ppermute | solution.py:31
  52.7 9.7 %collective-permute-start.11 = (bf16[128,512]{1,0:T(8,128)(2,1)S(1)}, bf16[128,512]{1,0:T(8,128)(2,1)S(1)}, u32[]{:S(2)}, u32[]{:S(2)}) collective-permute-start(bf16[128,512]{1,0:T(8,128)(2,1)S(1)} %get-tuple-element.76), channel_id=1, source_target_pairs={{0,6},{1,7},{2,4},{3,5},{4,2},{5,3},{6,0},{7,1},{8,14},{9,15},{10,... | collective-permute-start | bytes 393224 | tf_op jit(solution)/shard_map/ppermute | solution.py:31
  54.9 7.5 %collective-permute-start.12 = (bf16[128,512]{1,0:T(8,128)(2,1)S(1)}, bf16[128,512]{1,0:T(8,128)(2,1)S(1)}, u32[]{:S(2)}, u32[]{:S(2)}) collective-permute-start(bf16[128,512]{1,0:T(8,128)(2,1)S(1)} %get-tuple-element.77), channel_id=1, source_target_pairs={{0,1},{1,0},{2,3},{3,2},{4,5},{5,4},{6,7},{7,6},{8,9},{9,8},{10,11... | collective-permute-start | bytes 393224 | tf_op jit(solution)/shard_map/ppermute | solution.py:31
  66.3 9.3 %collective-permute-start.16 = (bf16[128,512]{1,0:T(8,128)(2,1)S(1)}, bf16[128,512]{1,0:T(8,128)(2,1)S(1)}, u32[]{:S(2)}, u32[]{:S(2)}) collective-permute-start(bf16[128,512]{1,0:T(8,128)(2,1)S(1)} %get-tuple-element.86), channel_id=1, source_target_pairs={{0,7},{1,2},{2,1},{3,4},{4,3},{5,6},{6,5},{7,0},{8,15},{9,10},{10,... | collective-permute-start | bytes 393224 | tf_op jit(solution)/shard_map/ppermute | solution.py:31
  67.3 8.3 %collective-permute-start.17 = (bf16[128,512]{1,0:T(8,128)(2,1)S(1)}, bf16[128,512]{1,0:T(8,128)(2,1)S(1)}, u32[]{:S(2)}, u32[]{:S(2)}) collective-permute-start(bf16[128,512]{1,0:T(8,128)(2,1)S(1)} %get-tuple-element.87), channel_id=1, source_target_pairs={{0,2},{1,3},{2,0},{3,1},{4,6},{5,7},{6,4},{7,5},{8,10},{9,11},{10,... | collective-permute-start | bytes 393224 | tf_op jit(solution)/shard_map/ppermute | solution.py:31
  68.4 7.5 %collective-permute-start.18 = (bf16[128,512]{1,0:T(8,128)(2,1)S(1)}, bf16[128,512]{1,0:T(8,128)(2,1)S(1)}, u32[]{:S(2)}, u32[]{:S(2)}) collective-permute-start(bf16[128,512]{1,0:T(8,128)(2,1)S(1)} %get-tuple-element.88), channel_id=1, source_target_pairs={{0,6},{1,7},{2,4},{3,5},{4,2},{5,3},{6,0},{7,1},{8,14},{9,15},{10,... | collective-permute-start | bytes 393224 | tf_op jit(solution)/shard_map/ppermute | solution.py:31
  68.8 7.2 %collective-permute-start.19 = (bf16[128,512]{1,0:T(8,128)(2,1)S(1)}, bf16[128,512]{1,0:T(8,128)(2,1)S(1)}, u32[]{:S(2)}, u32[]{:S(2)}) collective-permute-start(bf16[128,512]{1,0:T(8,128)(2,1)S(1)} %get-tuple-element.89), channel_id=1, source_target_pairs={{0,1},{1,0},{2,3},{3,2},{4,5},{5,4},{6,7},{7,6},{8,9},{9,8},{10,11... | collective-permute-start | bytes 393224 | tf_op jit(solution)/shard_map/ppermute | solution.py:31
